TPU v7x, 512 devices: a whole 4x8x8 slice. The times are simulated.
512 devices in a mesh: tm: 8 (over y_lo, core), rows: 64 (over x, z, y_hi).
Axes of the slice: x: 4, y: 8 (y_hi: 2, y_lo: 4; y = y_hi * 4 + y_lo), z: 8, core: 2. Of those that a mesh axis runs over, the one named last changes fastest.
Arguments:
- inputs: bfloat16 [16, 256, 16, 256], P('tm', 'rows'), may hold values from -6 to 6
- cotangent: bfloat16 [16, 256, 16, 256], P('tm', 'rows'), may hold values from -16 to 16
- kernel: bfloat16 [27, 256, 256], P(None, 'rows', 'tm'), may hold values from -0.078125 to 0.078125
Outputs:
- grad_inputs: bfloat16 [16, 256, 16, 256], P('tm', 'rows')
- grad_kernel: float32 [27, 256, 256], P(None, 'rows', 'tm')
All inputs are finite; a program needn't handle non-finite values.
Results may differ from a plain program's by a relative error of at most 0.003.
Values may be sent and summed in bfloat16 or wider, within the bound.
No kernel may reach another device: no remote copies, remote signals or barrier semaphores. Data moves between devices by JAX's collectives and lax.ppermute only.
A program may use at most 64 MiB of HBM per device.

v0:
```python
import jax
import jax.numpy as jnp
from jax import lax
from jax.sharding import PartitionSpec as P


def extended(block, sides, width):
    for axis, dim in sides:
        count = lax.axis_size(axis)
        forward = [(i, i + 1) for i in range(count - 1)]
        backward = [(target, source) for source, target in forward]
        low = lax.ppermute(
            lax.slice_in_dim(block, block.shape[dim] - width, None, axis=dim), axis, forward
        )
        high = lax.ppermute(lax.slice_in_dim(block, 0, width, axis=dim), axis, backward)
        block = jnp.concatenate([low, block, high], axis=dim)
    return block


def shifted(value, axis, steps):
    count = lax.axis_size(axis)
    leading, last = (max(0, -steps), min(count, count - steps))
    return lax.ppermute(value, axis, [(source, source + steps) for source in range(leading, last)])


def silu_slope(values):
    logistic = jax.nn.sigmoid(values)
    return logistic * (1.0 + values * (1.0 - logistic))


def widen_cols(values):
    return jnp.pad(values, ((0, 0), (0, 0), (1, 1), (0, 0)))


def tap_columns(padded, frames, height, across):
    pieces = []
    for time_tap in range(3):
        for row_tap in range(3):
            for col_tap in range(3):
                start_time, start_row, start_col = (2 - time_tap, 2 - row_tap, 2 - col_tap)
                pieces.append(
                    padded[
                        start_time : start_time + frames,
                        start_row : start_row + height,
                        start_col : start_col + across,
                    ]
                )
    stacked = jnp.stack(pieces, 3)
    return stacked.reshape(frames * height * across, 27, padded.shape[3])


def backward_piece(columns, portion):
    return lax.dot_general(
        columns, portion, (((1, 2), (0, 2)), ((), ())), preferred_element_type=jnp.float32
    )


def kernel_grad(haloed, gradient, factor):
    height = gradient.shape[1]
    across = gradient.shape[2]
    channels = haloed.shape[3]
    split_grads = lax.all_to_all(gradient, "tm", split_axis=3, concat_axis=0, tiled=True)
    width_out = split_grads.shape[3]
    padded_grads = jnp.pad(split_grads, ((0, 2), (0, 0), (0, 0), (0, 0)))
    portion = lax.all_gather(haloed, "tm", axis=0, tiled=True)
    offset = jnp.int32(0)
    portion_frames = portion.shape[0]
    widened = widen_cols(portion)
    spatial = jnp.stack(
        [
            widened[:, row_tap : row_tap + height, col_tap : col_tap + across]
            for row_tap in range(3)
            for col_tap in range(3)
        ],
        3,
    )
    shifted_grads = jnp.stack(
        [
            lax.dynamic_slice_in_dim(padded_grads, offset + 2 - time_tap, portion_frames, 0)
            for time_tap in range(3)
        ],
        0,
    )
    contribution = lax.dot_general(
        spatial,
        shifted_grads,
        (((0, 1, 2), (1, 2, 3)), ((), ())),
        preferred_element_type=jnp.float32,
    )
    contribution = jnp.transpose(contribution, (2, 0, 1, 3)).reshape(27, channels, width_out)
    return lax.psum_scatter(contribution * factor, "rows", scatter_dimension=1, tiled=True)


def local(inputs, cotangent, kernel):
    frames, height, across, channels = inputs.shape
    rows_kernel = lax.all_gather(kernel, "rows", axis=1, tiled=True)
    act = jax.nn.silu(inputs.astype(jnp.float32)).astype(jnp.bfloat16)
    paired = jnp.concatenate([act, cotangent], 3)
    paired_rows = extended(paired, (("rows", 1),), 1)
    halo_act = paired_rows[:, :, :, :channels]
    halo_grad = paired_rows[:, :, :, channels:]
    ahead_frames = jnp.concatenate([halo_grad, shifted(halo_grad, "tm", -1)], 0)
    cols_grad = tap_columns(widen_cols(ahead_frames), frames, height, across)
    grad_act = backward_piece(cols_grad, lax.all_gather(rows_kernel, "tm", axis=2, tiled=True))
    grad_act = grad_act.reshape(frames, height, across, channels)
    grad_inputs = (
        cotangent.astype(jnp.float32) + grad_act * silu_slope(inputs.astype(jnp.float32))
    ).astype(jnp.bfloat16)
    factor = float(frames * lax.axis_size("tm") * height * lax.axis_size("rows") * across) ** (-0.5)
    grad_kernel = kernel_grad(halo_act, cotangent, factor)
    return (grad_inputs, grad_kernel)


def solution(mesh):
    return jax.shard_map(
        local,
        mesh=mesh,
        in_specs=(P("tm", "rows", None, None), P("tm", "rows", None, None), P(None, "rows", "tm")),
        out_specs=(P("tm", "rows", None, None), P(None, "rows", "tm")),
        check_vma=False,
    )
```

profile of v0, /device:TPU:8, one launch (start us, length us, event | category | flops | bytes accessed | tf_op | source)
XLA Modules:
  0.0 590.8 jit_solution(595084361078024276)
XLA Ops:
  8.0 0.9 fusion.49
  8.9 0.7 pad_maximum_fusion.7
  9.6 1.3 collective-permute-start.1
  10.9 8.5 %collective-permute-start = (bf16[2,1,16,512]{3,2,1,0:T(8,128)(2,1)S(1)}, bf16[2,1,16,512]{3,2,1,0:T(8,128)(2,1)S(1)}, u32[]{:S(2)}, u32[]{:S(2)}) collective-permute-start(bf16[2,1,16,512]{3,2,1,0:T(8,128)(2,1)S(1)} %get-tuple-element.10), channel_id=1, source_target_pairs={{0,1},{1,2},{2,3},{3,4},{4,5},{5,6},{6,7},{7,8},{8,9},{9,10},{10,1... | collective-permute-start | bytes 98312 | tf_op jit(solution)/shard_map/ppermute | solution.py:12
  19.4 1.2 copy.88
  20.6 1.2 reshape.124
  21.7 9.1 %all-to-all-start = ((bf16[8,2,2048]{2,1,0:T(2,128)(2,1)}), bf16[8,2,2048]{2,1,0:T(2,128)(2,1)S(1)}, u32[]{:S(2)}, u32[]{:S(2)}) async-start(bf16[8,2,2048]{2,1,0:T(2,128)(2,1)} %reshape.124), calls=%async_computation | async-start | bytes 131072 | tf_op jit(solution)/shard_map/all_to_all | solution.py:62
  30.8 0.9 pad_maximum_fusion.1
  31.7 16.0 %all_gather.11 = bf16[16,6,16,256]{3,2,1,0:T(8,128)(2,1)S(1)} all-gather(bf16[2,6,16,256]{3,2,1,0:T(8,128)(2,1)S(1)} %get-tuple-element.8), channel_id=1, replica_groups=mesh['tm'=8,'rows'=64] {'tm'}, dimensions={0}, use_global_device_ids=true | all-gather | bytes 884736 | tf_op jit(solution)/shard_map/all_gather | solution.py:65
  47.7 0.9 fusion.30
  48.6 0.8 fusion.43
  49.5 1.0 fusion.32
  50.5 1.0 fusion.34
  51.5 0.8 fusion.42
  52.3 1.0 fusion.36
  53.3 1.0 fusion.38
  54.3 0.8 fusion.41
  55.2 1.0 fusion.40
  56.2 0.4 reshape.125
  56.5 0.3 copy.89
  56.9 0.1 fusion.44
  57.0 3.3 fusion.10
  60.4 4.4 copy.91
  64.9 0.7 copy-done.2
  65.5 311.1 %all_gather.9 = bf16[27,256,32]{2,0,1:T(8,128)(2,1)S(1)} all-gather(bf16[27,4,32]{2,0,1:T(8,128)(2,1)S(1)} %copy.86), channel_id=1, replica_groups=mesh['tm'=8,'rows'=64] {'rows'}, dimensions={1}, use_global_device_ids=true | all-gather | bytes 449280 | tf_op jit(solution)/shard_map/all_gather | solution.py:96
  376.7 2.6 copy.87
  379.3 1.9 collective-permute-start.2
  381.2 2.7 collective-permute-done.2
  384.3 0.5 copy-done
  385.0 193.5 %reduce-scatter.2.cloned.1.call-done = f32[27,4,32]{2,0,1:T(8,128)} async-done(((f32[27,256,32]{2,0,1:T(8,128)}), f32[27,4,32]{2,0,1:T(8,128)}) %reduce-scatter.2.cloned.1.call-update) | async-done | bytes 13840 | tf_op jit(solution)/shard_map/reduce_scatter | solution.py:91
  578.5 1.5 copy.92
  580.0 3.3 fusion.22
  (43 shorter events, 0.6 us)
Async XLA Ops:
  9.6 21.2 %collective-permute-start.1 = (bf16[2,1,16,512]{3,2,1,0:T(8,128)(2,1)S(1)}, bf16[2,1,16,512]{3,2,1,0:T(8,128)(2,1)S(1)}, u32[]{:S(2)}, u32[]{:S(2)}) collective-permute-start(bf16[2,1,16,512]{3,2,1,0:T(8,128)(2,1)S(1)} %get-tuple-element.11), channel_id=1, source_target_pairs={{1,0},{2,1},{3,2},{4,3},{5,4},{6,5},{7,6},{8,7},{9,8},{10,9},{11,1... | collective-permute-start | bytes 98312 | tf_op jit(solution)/shard_map/ppermute | solution.py:15
  10.9 19.9 %collective-permute-start = (bf16[2,1,16,512]{3,2,1,0:T(8,128)(2,1)S(1)}, bf16[2,1,16,512]{3,2,1,0:T(8,128)(2,1)S(1)}, u32[]{:S(2)}, u32[]{:S(2)}) collective-permute-start(bf16[2,1,16,512]{3,2,1,0:T(8,128)(2,1)S(1)} %get-tuple-element.10), channel_id=1, source_target_pairs={{0,1},{1,2},{2,3},{3,4},{4,5},{5,6},{6,7},{7,8},{8,9},{9,10},{10,1... | collective-permute-start | bytes 98312 | tf_op jit(solution)/shard_map/ppermute | solution.py:12
  21.7 34.4 %all-to-all-start = ((bf16[8,2,2048]{2,1,0:T(2,128)(2,1)}), bf16[8,2,2048]{2,1,0:T(2,128)(2,1)S(1)}, u32[]{:S(2)}, u32[]{:S(2)}) async-start(bf16[8,2,2048]{2,1,0:T(2,128)(2,1)} %reshape.124), calls=%async_computation | async-start | bytes 131072 | tf_op jit(solution)/shard_map/all_to_all | solution.py:62
  30.8 547.7 %reduce-scatter.2.cloned.1.call-start = ((), (), s32[]{:S(2)}) async-start(), calls=%async_computation.3 | async-start | bytes 4259840 | tf_op jit(solution)/shard_map/reduce_scatter | solution.py:91
  64.8 0.7 copy-start.2
  64.8 515.2 %all-gather.2.cloned.1.call-start = ((), (), s32[]{:S(2)}) async-start(), calls=%async_computation.2 | async-start | bytes 3981312 | tf_op jit(solution)/shard_map/all_gather | solution.py:104
  379.3 4.6 collective-permute-start.2
  384.0 0.8 copy-start
  384.2 195.9 %copy-start.1 = (bf16[2,4,16,256]{3,2,1,0:T(8,128)(2,1)S(1)}, bf16[2,4,16,256]{3,2,1,0:T(8,128)(2,1)}, u32[]{:S(2)}) copy-start(bf16[2,4,16,256]{3,2,1,0:T(8,128)(2,1)} %param.3) | copy-start | bytes 196612
Sparse Core Ops, SparseCore 0:
  64.9 513.5 reduce-scatter.1
Sparse Core Ops, SparseCore 1:
  379.3 67.6 all-gather.1
where the time goes:
time: 591 us
  blocking collectives  327 us (55%)
  waiting for transfers between devices  196 us (33%)
  local copies, waits for them, and re-layouts  21.7 us (4%)
  starting transfers between devices  20.8 us (4%)
  between operations  15.8 us (3%)
  matrix products  6.58 us (1%)
    all_gather x1, blocking collectives, local(): rows_kernel = lax.all_gather(kernel, 'rows', axis=1, tiled=True)  311 us
    reduce_scatter x1, waiting for transfers between devices, kernel_grad(): lax.psum_scatter(contribution * factor, 'rows', scatter_dimension=1, tile...  194 us
    all_gather x1, blocking collectives, kernel_grad(): portion = lax.all_gather(haloed, 'tm', axis=0, tiled=True)  16 us
    unnamed x40, local copies, waits for them, and re-layouts  13.2 us
  transfers between devices with their start and end apart: 6, of which 2 were waited for; matrix products, arithmetic and copies ran while one was open for 3% of the time, Pallas kernels for 0%

commit v1 on v0

v1 whole, which is shorter than its diff:
```python
import jax
import jax.numpy as jnp
from jax import lax
from jax.sharding import PartitionSpec as P


def silu_slope(values):
    logistic = jax.nn.sigmoid(values)
    return logistic * (1.0 + values * (1.0 - logistic))


def exchanged(blocks, axis):
    return lax.all_to_all(blocks, axis, split_axis=0, concat_axis=0, tiled=True)


def with_halo_rows(block):
    count = lax.axis_size("rows")
    forward = [(i, i + 1) for i in range(count - 1)]
    backward = [(target, source) for source, target in forward]
    above = lax.ppermute(block[:, -1:], "rows", forward)
    below = lax.ppermute(block[:, :1], "rows", backward)
    return jnp.concatenate([above, block, below], axis=1)


def tap_windows(padded, frames, height, across):
    pieces = [
        padded[2 - t : 2 - t + frames, 2 - r : 2 - r + height, 2 - c : 2 - c + across]
        for t in range(3)
        for r in range(3)
        for c in range(3)
    ]
    return jnp.concatenate(pieces, axis=3)


def local(inputs, cotangent, kernel):
    frames, height, across, channels = inputs.shape
    groups = lax.axis_size("tm")
    bands = lax.axis_size("rows")
    taps, own_in, own_out = kernel.shape
    points = frames * height * across

    own_kernel = jnp.transpose(kernel, (1, 0, 2)).reshape(1, own_in, taps * own_out)
    kernel_in = exchanged(jnp.broadcast_to(own_kernel, (bands, own_in, taps * own_out)), "rows")
    kernel_in = kernel_in.reshape(bands * own_in, taps * own_out)

    act = jax.nn.silu(inputs.astype(jnp.float32)).astype(jnp.bfloat16)
    act_all = lax.all_gather(act.reshape(points, channels), "tm", axis=0, tiled=True)

    haloed = with_halo_rows(cotangent)
    split = haloed.reshape(frames, height + 2, across, groups, own_out).transpose(3, 0, 1, 2, 4)
    grads = exchanged(split, "tm").reshape(groups * frames, height + 2, across, own_out)
    padded = jnp.pad(grads, ((0, 2), (0, 0), (1, 1), (0, 0)))
    windows = tap_windows(padded, groups * frames, height, across)
    windows = windows.reshape(groups * points, taps * own_out)

    factor = float(points * groups * bands) ** (-0.5)
    terms = lax.dot_general(
        act_all, windows, (((0,), (0,)), ((), ())), preferred_element_type=jnp.float32
    )
    terms = (terms * factor).astype(jnp.bfloat16).reshape(bands, own_in, taps * own_out)
    grad_kernel = jnp.sum(exchanged(terms, "rows").astype(jnp.float32), axis=0)
    grad_kernel = grad_kernel.reshape(own_in, taps, own_out).transpose(1, 0, 2)

    partial = lax.dot_general(
        windows, kernel_in, (((1,), (1,)), ((), ())), preferred_element_type=jnp.float32
    )
    partial = partial.astype(jnp.bfloat16).reshape(groups, points, channels)
    grad_act = jnp.sum(exchanged(partial, "tm").astype(jnp.float32), axis=0)
    grad_act = grad_act.reshape(inputs.shape)
    grad_inputs = (
        cotangent.astype(jnp.float32) + grad_act * silu_slope(inputs.astype(jnp.float32))
    ).astype(jnp.bfloat16)
    return (grad_inputs, grad_kernel)


def solution(mesh):
    return jax.shard_map(
        local,
        mesh=mesh,
        in_specs=(P("tm", "rows", None, None), P("tm", "rows", None, None), P(None, "rows", "tm")),
        out_specs=(P("tm", "rows", None, None), P(None, "rows", "tm")),
        check_vma=False,
    )
```

time: 591 us -> 132 us (0.22)
  the two profiles are of different devices: /device:TPU:8 before, /device:TPU:16 now
where the time goes in v1:
time: 132 us; the launch traced here: 131 us
  blocking collectives  60 us (45%)
  starting transfers between devices  29.6 us (22%)
  waiting for transfers between devices  21.6 us (16%)
  local copies, waits for them, and re-layouts  15.9 us (12%)
  other arithmetic  1.85 us (1%)
  matrix products  1.6 us (1%)
    all_to_all x2, blocking collectives, exchanged(): return lax.all_to_all(blocks, axis, split_axis=0, concat_axis=0, tiled=True)  44 us
    all_to_all x2, starting transfers between devices, exchanged(): return lax.all_to_all(blocks, axis, split_axis=0, concat_axis=0, tiled=True)  22.4 us
    all_gather x1, blocking collectives, local(): lax.all_gather(act.reshape(points, channels), 'tm', axis=0, tiled=True)  15.9 us
    all_to_all x2, waiting for transfers between devices, exchanged(): return lax.all_to_all(blocks, axis, split_axis=0, concat_axis=0, tiled=True)  13.4 us
    ppermute x1, waiting for transfers between devices, with_halo_rows(): below = lax.ppermute(block[:, :1], 'rows', backward)  8.13 us
    concatenate x1, local copies, waits for them, and re-layouts, tap_windows(): return jnp.concatenate(pieces, axis=3)  6.99 us
    ppermute x1, starting transfers between devices, with_halo_rows(): above = lax.ppermute(block[:, -1:], 'rows', forward)  5.92 us
    slice x2, local copies, waits for them, and re-layouts, tap_windows(): padded[2 - t:2 - t + frames, 2 - r:2 - r + height, 2 - c:2 - c + across]  4.28 us
  transfers between devices with their start and end apart: 4, of which 4 were waited for; matrix products, arithmetic and copies ran while one was open for 9% of the time, Pallas kernels for 0%

profile of v1, /device:TPU:16, one launch (start us, length us, event | category | flops | bytes accessed | tf_op | source)
XLA Modules:
  0.0 131.2 jit_solution(12827935210573969307)
XLA Ops:
  0.6 0.7 fusion.11
  1.4 5.9 %collective-permute-start = (bf16[2,1,16,256]{3,2,1,0:T(8,128)(2,1)S(1)}, bf16[2,1,16,256]{3,2,1,0:T(8,128)(2,1)S(1)}, u32[]{:S(2)}, u32[]{:S(2)}) collective-permute-start(bf16[2,1,16,256]{3,2,1,0:T(8,128)(2,1)S(1)} %get-tuple-element.37), channel_id=1, source_target_pairs={{0,1},{1,2},{2,3},{3,4},{4,5},{5,6},{6,7},{7,8},{8,9},{9,10},{10,1... | collective-permute-start | bytes 49160 | tf_op jit(solution)/shard_map/ppermute | solution.py:20
  7.3 1.3 collective-permute-start.1
  8.6 0.1 collective-permute-done
  8.7 8.1 %collective-permute-done.1 = bf16[2,1,16,256]{3,2,1,0:T(8,128)(2,1)S(1)} collective-permute-done((bf16[2,1,16,256]{3,2,1,0:T(8,128)(2,1)S(1)}, bf16[2,1,16,256]{3,2,1,0:T(8,128)(2,1)S(1)}, u32[]{:S(2)}, u32[]{:S(2)}) %collective-permute-start.1) | collective-permute-done | bytes 16416 | tf_op jit(solution)/shard_map/ppermute | solution.py:21
  16.9 0.9 pad_maximum_fusion
  17.7 0.2 reshape.33
  17.9 0.1 copy.12
  18.0 1.0 reshape.42
  19.0 5.4 %all-to-all-start = ((bf16[8,2,3072]{2,1,0:T(2,128)(2,1)}), bf16[8,2,3072]{2,1,0:T(2,128)(2,1)S(1)}, u32[]{:S(2)}, u32[]{:S(2)}) async-start(bf16[8,2,3072]{2,1,0:T(2,128)(2,1)} %reshape.42), calls=%async_computation | async-start | bytes 196608 | tf_op jit(solution)/shard_map/all_to_all | solution.py:13
  24.4 0.1 broadcast_in_dim.7
  24.5 3.7 %all-to-all-done = bf16[8,2,3072]{2,1,0:T(2,128)(2,1)S(1)} async-done(((bf16[8,2,3072]{2,1,0:T(2,128)(2,1)}), bf16[8,2,3072]{2,1,0:T(2,128)(2,1)S(1)}, u32[]{:S(2)}, u32[]{:S(2)}) %all-to-all-start) | async-done | bytes 98336 | tf_op jit(solution)/shard_map/all_to_all | solution.py:13
  28.3 0.9 broadcast_in_dim.8
  29.1 17.0 %all-to-all-start.1 = ((bf16[64,4,864]{2,1,0:T(4,128)(2,1)}), bf16[64,4,864]{2,1,0:T(4,128)(2,1)S(1)}, u32[]{:S(2)}, u32[]{:S(2)}) async-start(bf16[64,4,864]{2,1,0:T(4,128)(2,1)} %broadcast_in_dim.8), calls=%async_computation.1 | async-start | bytes 917504 | tf_op jit(solution)/shard_map/all_to_all | solution.py:13
  46.1 0.2 reshape.43
  46.3 3.0 %pad_slice_fusion = (bf16[16,4,16,32]{3,2,1,0:T(8,128)(2,1)}, bf16[16,4,16,32]{3,2,1,0:T(8,128)(2,1)}, bf16[16,4,16,32]{3,2,1,0:T(8,128)(2,1)}, bf16[16,4,16,32]...) fusion(bf16[16,6,16,32]{3,2,1,0:T(8,128)(2,1)S(1)} %bitcast.14), kind=kLoop, calls=%fused_computation | loop fusion | bytes 1343488 | tf_op jit(solution)/shard_map/slice | solution.py:27
  49.3 1.3 %fusion.10 = (bf16[16,4,16,32]{3,2,1,0:T(8,128)(2,1)S(1)}, bf16[16,4,16,32]{3,2,1,0:T(8,128)(2,1)S(1)}, bf16[16,4,16,32]{3,2,1,0:T(8,128)(2,1)S(1)}, bf16[16,4,1...) fusion(bf16[16,6,16,32]{3,2,1,0:T(8,128)(2,1)S(1)} %bitcast.15), kind=kLoop, calls=%fused_computation.42 | loop fusion | bytes 1703936 | tf_op jit(solution)/shard_map/slice | solution.py:27
  50.6 7.0 %concatenate.7 = bf16[16,4,16,864]{3,2,1,0:T(8,128)(2,1)S(1)} concatenate(bf16[16,4,16,32]{3,2,1,0:T(8,128)(2,1)} %get-tuple-element.34, bf16[16,4,16,32]{3,2,1,0:T(8,128)(2,1)} %get-tuple-element.9, bf16[16,4,16,32]{3,2,1,0:T(8,128)(2,1)} %get-tuple-element.10, bf16[16,4,16,32]{3,2,1,0:T(8,128)(2,1)} %get-tuple-element.11, bf16[16,4,16,32]{3,2,1,0:T(8,128)(2,1)} %get-tuple-element.12, ...), dimensions={3} | concatenate | bytes 3538944 | tf_op jit(solution)/shard_map/concatenate | solution.py:32
  57.6 9.6 %all-to-all-done.1 = bf16[64,4,864]{2,1,0:T(4,128)(2,1)S(1)} async-done(((bf16[64,4,864]{2,1,0:T(4,128)(2,1)}), bf16[64,4,864]{2,1,0:T(4,128)(2,1)S(1)}, u32[]{:S(2)}, u32[]{:S(2)}) %all-to-all-start.1) | async-done | bytes 442400 | tf_op jit(solution)/shard_map/all_to_all | solution.py:13
  67.3 0.2 reshape.36
  67.5 0.7 convolution_convert_fusion
  68.3 16.6 %all_to_all.20 = bf16[8,128,256]{2,1,0:T(8,128)(2,1)S(1)} all-to-all(bf16[8,128,256]{2,1,0:T(8,128)(2,1)S(1)} %bitcast.20), channel_id=1, replica_groups=mesh['tm'=8,'rows'=64] {'tm'}, dimensions={0} | all-to-all | bytes 1048576 | tf_op jit(solution)/shard_map/all_to_all | solution.py:13
  84.8 0.1 convert_reduce_fusion
  84.9 0.7 fusion.9
  85.6 15.9 %all_gather.3 = bf16[1024,256]{1,0:T(8,128)(2,1)S(1)} all-gather(bf16[128,256]{1,0:T(8,128)(2,1)S(1)} %bitcast.21), channel_id=1, replica_groups=mesh['tm'=8,'rows'=64] {'tm'}, dimensions={0}, use_global_device_ids=true | all-gather | bytes 589824 | tf_op jit(solution)/shard_map/all_gather | solution.py:47
  101.6 0.9 fusion
  102.4 0.2 copy.14
  102.7 0.1 reshape.40
  102.8 27.5 %all_to_all.21 = bf16[64,4,864]{2,1,0:T(4,128)(2,1)S(1)} all-to-all(bf16[64,4,864]{2,1,0:T(4,128)(2,1)S(1)} %reshape.40), channel_id=1, replica_groups=mesh['tm'=8,'rows'=64] {'rows'}, dimensions={0} | all-to-all | bytes 884736 | tf_op jit(solution)/shard_map/all_to_all | solution.py:13
  130.3 0.2 convert_reduce_fusion.1
  130.5 0.1 reshape.41
  130.6 0.7 copy.15
  (7 shorter events, 0.0 us)
Async XLA Ops:
  0.6 23.8 %copy-start.2 = (bf16[27,4,32]{2,1,0:T(4,128)(2,1)S(1)}, bf16[27,4,32]{2,1,0:T(4,128)(2,1)}, u32[]{:S(2)}) copy-start(bf16[27,4,32]{2,1,0:T(4,128)(2,1)} %param.5) | copy-start | bytes 20740
  1.4 7.4 %collective-permute-start = (bf16[2,1,16,256]{3,2,1,0:T(8,128)(2,1)S(1)}, bf16[2,1,16,256]{3,2,1,0:T(8,128)(2,1)S(1)}, u32[]{:S(2)}, u32[]{:S(2)}) collective-permute-start(bf16[2,1,16,256]{3,2,1,0:T(8,128)(2,1)S(1)} %get-tuple-element.37), channel_id=1, source_target_pairs={{0,1},{1,2},{2,3},{3,4},{4,5},{5,6},{6,7},{7,8},{8,9},{9,10},{10,1... | collective-permute-start | bytes 49160 | tf_op jit(solution)/shard_map/ppermute | solution.py:20
  7.3 9.6 %collective-permute-start.1 = (bf16[2,1,16,256]{3,2,1,0:T(8,128)(2,1)S(1)}, bf16[2,1,16,256]{3,2,1,0:T(8,128)(2,1)S(1)}, u32[]{:S(2)}, u32[]{:S(2)}) collective-permute-start(bf16[2,1,16,256]{3,2,1,0:T(8,128)(2,1)S(1)} %get-tuple-element.38), channel_id=1, source_target_pairs={{1,0},{2,1},{3,2},{4,3},{5,4},{6,5},{7,6},{8,7},{9,8},{10,9},{11,1... | collective-permute-start | bytes 49160 | tf_op jit(solution)/shard_map/ppermute | solution.py:21
  19.0 9.2 %all-to-all-start = ((bf16[8,2,3072]{2,1,0:T(2,128)(2,1)}), bf16[8,2,3072]{2,1,0:T(2,128)(2,1)S(1)}, u32[]{:S(2)}, u32[]{:S(2)}) async-start(bf16[8,2,3072]{2,1,0:T(2,128)(2,1)} %reshape.42), calls=%async_computation | async-start | bytes 196608 | tf_op jit(solution)/shard_map/all_to_all | solution.py:13
  29.1 38.1 %all-to-all-start.1 = ((bf16[64,4,864]{2,1,0:T(4,128)(2,1)}), bf16[64,4,864]{2,1,0:T(4,128)(2,1)S(1)}, u32[]{:S(2)}, u32[]{:S(2)}) async-start(bf16[64,4,864]{2,1,0:T(4,128)(2,1)} %broadcast_in_dim.8), calls=%async_computation.1 | async-start | bytes 917504 | tf_op jit(solution)/shard_map/all_to_all | solution.py:13
  67.5 17.4 %copy-start = (bf16[2,4,16,256]{3,2,1,0:T(8,128)(2,1)S(1)}, bf16[2,4,16,256]{3,2,1,0:T(8,128)(2,1)}, u32[]{:S(2)}) copy-start(bf16[2,4,16,256]{3,2,1,0:T(8,128)(2,1)} %param.4) | copy-start | bytes 196612
  67.5 17.4 %copy-start.1 = (bf16[2,4,16,256]{3,2,1,0:T(8,128)(2,1)S(1)}, bf16[2,4,16,256]{3,2,1,0:T(8,128)(2,1)}, u32[]{:S(2)}) copy-start(bf16[2,4,16,256]{3,2,1,0:T(8,128)(2,1)} %param.3) | copy-start | bytes 196612

commit v2 on v1

v2 whole, which is shorter than its diff:
```python
import jax
import jax.numpy as jnp
from jax import lax
from jax.experimental import pallas as pl
from jax.experimental.pallas import tpu as pltpu
from jax.sharding import PartitionSpec as P


BF16 = jnp.bfloat16
F32 = jnp.float32
CHIPS = 4
CORES = 2
GROUPS = CHIPS * CORES
FAR = 4
OWN = 32
TAPS = 27
LANES = 128
SLOT = 896
WIDE = 9 * LANES


def chip_and_core():
    me = lax.axis_index("tm")
    return me // CORES, me % CORES


def called(body, outs, *args, scratch=(), flops=0, limit=24):
    whole = pl.BlockSpec(memory_space=pltpu.VMEM)
    size = sum(a.size * a.dtype.itemsize for a in (*args, *outs))
    return pl.pallas_call(
        body,
        out_shape=outs,
        in_specs=[whole] * len(args),
        out_specs=[whole] * len(outs),
        scratch_shapes=scratch,
        compiler_params=pltpu.CompilerParams(vmem_limit_bytes=limit << 20),
        cost_estimate=pl.CostEstimate(flops=flops, bytes_accessed=size, transcendentals=0),
    )(*args)


def array(shape, dtype=BF16):
    return jax.ShapeDtypeStruct(shape, dtype)


def prepare(kernel_ref, inputs_ref, cot_ref, blocks_ref, above_ref, below_ref, body_ref):
    own_in = kernel_ref.shape[1]
    _, channels = inputs_ref.shape[2:]
    above_ref[...] = cot_ref[:, cot_ref.shape[1] - 1]
    below_ref[...] = cot_ref[:, 0]
    body_ref[:, :channels] = jnp.broadcast_to(
        jax.nn.silu(inputs_ref[...].reshape(-1, channels).astype(F32)).T.astype(BF16)[None],
        (CHIPS, channels, LANES),
    )
    halves = [cot_ref[frame].reshape(-1, channels).astype(F32) for frame in range(2)]
    for target in range(CHIPS):
        body_ref[target, channels:] = for_chip(target, *halves)
    pieces = [kernel_ref[tap].astype(F32) for tap in range(TAPS)]
    pieces.append(jnp.zeros((own_in, SLOT - TAPS * OWN), F32))
    slot = jnp.concatenate(pieces, axis=1).astype(BF16)
    blocks_ref[...] = jnp.broadcast_to(slot[None], blocks_ref.shape)


def for_chip(target, first, second):
    tile = slice(LANES * (target // 2), LANES * (target // 2) + LANES)
    first, second = first[:, tile], second[:, tile]
    low = lax.broadcasted_iota(jnp.int32, first.shape, 1) < LANES // 2
    if target % 2 == 0:
        second = pltpu.roll(second, LANES // 2, 1)
    else:
        first = pltpu.roll(first, LANES // 2, 1)
    return jnp.where(low, first, second).astype(BF16)


def pack(body_ref, above_ref, below_ref, *out_and_scratch):
    outs, halo = out_and_scratch[:CHIPS], out_and_scratch[CHIPS]
    chip, _ = chip_and_core()
    rows = body_ref.shape[1]
    across = above_ref.shape[1]
    for side, ref in enumerate((above_ref, below_ref)):
        halves = [ref[frame].astype(F32) for frame in range(2)]
        for target in range(CHIPS):
            halo[target, across * side : across * side + across] = for_chip(target, *halves)
    for step, out in enumerate(outs):
        out[:rows] = body_ref[chip ^ step]
        out[rows:] = halo[chip ^ step]


def windows_and_terms(factor, all_ref, terms_ref, windows_ref, act, padded):
    chip, core = chip_and_core()
    channels = act.shape[0]
    across = 16
    height = 4
    span = (height + 2) * across
    row = lax.broadcasted_iota(jnp.int32, (LANES, LANES), 0)
    lane = lax.broadcasted_iota(jnp.int32, (LANES, LANES), 1)
    place = lax.broadcasted_iota(jnp.int32, (span, LANES), 0) % across
    group = lax.broadcasted_iota(jnp.int32, (span, LANES), 1) // OWN
    padded[2 * GROUPS :] = jnp.zeros((2, span, LANES), BF16)
    for other in range(CORES):
        for step in range(CHIPS):
            owner = CORES * (chip ^ step) + other
            act[:, pl.ds(pl.multiple_of(owner * LANES, LANES), LANES)] = all_ref[other, step, :channels]
            block = all_ref[other, step, channels:]
            held = span - 2 * across
            block = jnp.concatenate([block[held : held + across], block[:held], block[held + across :]], axis=0)
            for frame in range(2):
                chosen = (row == 64 * frame + OWN * core + lane % OWN).astype(F32).astype(BF16)
                copies = jnp.dot(block, chosen, preferred_element_type=F32)
                after = jnp.where(place == across - 1, 0.0, pltpu.roll(copies, span - 1, 0))
                before = jnp.where(place == 0, 0.0, pltpu.roll(copies, 1, 0))
                joined = jnp.where(group == 0, after, jnp.where(group == 1, copies, before))
                joined = jnp.where(group == 3, 0.0, joined)
                padded[CORES * owner + frame] = joined.astype(BF16)
    for time_tap in range(3):
        for row_tap in range(3):
            part = padded[2 - time_tap : 2 - time_tap + 2 * GROUPS, across * (2 - row_tap) : across * (2 - row_tap + height)]
            index = 3 * time_tap + row_tap
            windows_ref[:, LANES * index : LANES * index + LANES] = part.reshape(-1, LANES)
    terms = jnp.dot(act[...], windows_ref[...], preferred_element_type=F32) * factor
    pieces = [terms[:, LANES * index : LANES * index + 3 * OWN] for index in range(9)]
    pieces.append(jnp.zeros((channels, SLOT - TAPS * OWN), F32))
    terms = jnp.concatenate(pieces, axis=1)
    terms_ref[...] = terms.reshape(terms_ref.shape).astype(BF16)


def transposed(windows_ref, kernel_ref, keep_ref, give_ref, wide, product):
    chip, core = chip_and_core()
    bands, own_in, _ = kernel_ref.shape
    flat = kernel_ref[...].astype(F32).reshape(bands * own_in, SLOT)
    for index in range(9):
        wide[:, LANES * index : LANES * index + LANES] = flat[:, 3 * OWN * index : 3 * OWN * index + LANES].astype(BF16)
    product[...] = lax.dot_general(
        windows_ref[...], wide[...], (((1,), (1,)), ((), ())), preferred_element_type=F32
    ).reshape(product.shape)
    for step in range(CHIPS):
        keep_ref[step] = product[CORES * (chip ^ step) + core]
        give_ref[step] = product[CORES * (chip ^ step) + 1 - core].astype(BF16)


def paired(keep_ref, given_ref, own_ref, *outs):
    own_ref[...] = keep_ref[0] + given_ref[0].astype(F32)
    for step, out in enumerate(outs, 1):
        out[...] = (keep_ref[step] + given_ref[step].astype(F32)).astype(BF16)


def finish(own_ref, first_ref, second_ref, third_ref, inputs_ref, cot_ref, out_ref):
    total = own_ref[...] + first_ref[...].astype(F32) + second_ref[...].astype(F32) + third_ref[...].astype(F32)
    total = total.reshape(inputs_ref.shape)
    values = inputs_ref[...].astype(F32)
    logistic = jax.nn.sigmoid(values)
    slope = logistic * (1.0 + values * (1.0 - logistic))
    out_ref[...] = (cot_ref[...].astype(F32) + total * slope).astype(BF16)


def summed(terms_ref, out_ref):
    total = jnp.sum(terms_ref[...].astype(F32), axis=0)
    for tap in range(TAPS):
        out_ref[tap] = total[:, OWN * tap : OWN * tap + OWN]


def stepped(block, step):
    count = GROUPS
    return lax.ppermute(block, "tm", [(i, i ^ step) for i in range(count)])


def near_and_far(bands):
    near = bands // FAR
    return (
        [[near * x + i for i in range(near)] for x in range(FAR)],
        [[near * x + i for x in range(FAR)] for i in range(near)],
    )


def exchanged(blocks, groups):
    return lax.all_to_all(
        blocks, "rows", split_axis=0, concat_axis=0, tiled=True, axis_index_groups=groups
    )


def local(inputs, cotangent, kernel):
    frames, height, across, channels = inputs.shape
    bands = lax.axis_size("rows")
    own_in = kernel.shape[1]
    points = frames * height * across

    held = height * across
    blocks, above, below, body = called(
        prepare,
        [
            array((bands // FAR, own_in, SLOT)), array((frames, across, channels)),
            array((frames, across, channels)), array((CHIPS, channels + held, LANES)),
        ],
        kernel, inputs, cotangent, limit=60,
    )
    forward = [(i, i + 1) for i in range(bands - 1)]
    above = lax.ppermute(above, "rows", forward)
    below = lax.ppermute(below, "rows", [(b, a) for a, b in forward])

    near, far = near_and_far(bands)
    blocks = exchanged(blocks, near)
    blocks = jnp.broadcast_to(blocks[None], (FAR, *blocks.shape))
    kernel_in = exchanged(blocks, far).reshape(bands, own_in, SLOT)

    span = (height + 2) * across
    payload = array((channels + span, LANES))
    packs = called(
        pack, [payload] * CHIPS, body, above, below,
        scratch=[pltpu.VMEM((CHIPS, 2 * across, LANES), BF16)],
    )
    packs = [packs[0]] + [stepped(packs[step], CORES * step) for step in range(1, CHIPS)]
    every = lax.all_gather(jnp.stack(packs), "tm", axis=0, axis_index_groups=[[2 * i, 2 * i + 1] for i in range(CHIPS)])

    factor = float(points * GROUPS * bands) ** (-0.5)

    def terms_body(*refs):
        windows_and_terms(factor, *refs)

    terms, windows = called(
        terms_body, [array((bands, own_in, SLOT)), array((GROUPS * points, WIDE))], every,
        scratch=[pltpu.VMEM((channels, GROUPS * points), BF16), pltpu.VMEM((frames * GROUPS + 2, span, LANES), BF16)],
        flops=2 * GROUPS * points * WIDE * channels,
    )
    terms = exchanged(terms, None)

    keep, give = called(
        transposed, [array((CHIPS, points, channels), F32), array((CHIPS, points, channels))],
        windows, kernel_in,
        scratch=[pltpu.VMEM((channels, WIDE), BF16), pltpu.VMEM((GROUPS, points, channels), F32)],
        flops=2 * GROUPS * points * WIDE * channels,
    )
    given = stepped(give, 1)
    own, *sums = called(
        paired, [array((points, channels), F32)] + [array((points, channels))] * 3, keep, given
    )
    sums = [stepped(part, CORES * step) for step, part in enumerate(sums, 1)]
    grad_inputs, = called(finish, [array(inputs.shape)], own, *sums, inputs, cotangent)
    grad_kernel, = called(summed, [array(kernel.shape, F32)], terms)
    return (grad_inputs, grad_kernel)


def solution(mesh):
    return jax.shard_map(
        local,
        mesh=mesh,
        in_specs=(P("tm", "rows", None, None), P("tm", "rows", None, None), P(None, "rows", "tm")),
        out_specs=(P("tm", "rows", None, None), P(None, "rows", "tm")),
        check_vma=False,
    )
```

time: 132 us -> 92 us (0.70)
  the two profiles are of different devices: /device:TPU:16 before, /device:TPU:62 now
where the time goes in v2:
time: 92 us; the launch traced here: 91.3 us
  starting transfers between devices  67.6 us (73%)
  waiting for transfers between devices  11.8 us (13%)
  Pallas kernels  6.14 us (7%)
  local copies, waits for them, and re-layouts  2.64 us (3%)
  blocking collectives  2.32 us (3%)
    all_to_all x3, starting transfers between devices, exchanged(): lax.all_to_all(blocks, 'rows', split_axis=0, concat_axis=0, tiled=True, a...  35.7 us
    ppermute x7, starting transfers between devices, stepped(): return lax.ppermute(block, 'tm', [(i, i ^ step) for i in range(count)])  22.1 us
    ppermute x7, waiting for transfers between devices, stepped(): return lax.ppermute(block, 'tm', [(i, i ^ step) for i in range(count)])  6.64 us
    ppermute x1, starting transfers between devices, local(): below = lax.ppermute(below, 'rows', [(b, a) for a, b in forward])  6.38 us
    pallas_call x7, Pallas kernels, called(): pl.pallas_call(body, out_shape=outs, in_specs=[whole] * len(args), out_sp...  6.14 us
    ppermute x1, waiting for transfers between devices, local(): below = lax.ppermute(below, 'rows', [(b, a) for a, b in forward])  4.25 us
    ppermute x1, starting transfers between devices, local(): above = lax.ppermute(above, 'rows', forward)  3.36 us
    all_gather x1, blocking collectives, local(): lax.all_gather(jnp.stack(packs), 'tm', axis=0, axis_index_groups=[[2 * i,...  2.32 us
  transfers between devices with their start and end apart: 12, of which 5 were waited for; matrix products, arithmetic and copies ran while one was open for 1% of the time, Pallas kernels for 4%

profile of v2, /device:TPU:62, one launch (start us, length us, event | category | flops | bytes accessed | tf_op | source)
XLA Modules:
  0.0 91.3 jit_solution(16118344468833943731)
XLA Ops:
  0.6 1.8 %shard_map.50 = (bf16[16,4,896]{2,1,0:T(4,128)(2,1)}, bf16[2,16,256]{2,1,0:T(8,128)(2,1)}, bf16[2,16,256]{2,1,0:T(8,128)(2,1)}, bf16[4,320,128]{2,1,0:T(8,128)(2,1)}) custom-call(bf16[27,4,32]{2,1,0:T(4,128)(2,1)} %kernel_ref.1, bf16[2,4,16,256]{3,2,1,0:T(8,128)(2,1)} %inputs_ref.3, bf16[2,4,16,256]{3,2,1,0:T(8,128)(2,1)} %cot_ref.3), custom_call_target="tpu_custom_call" | custom-call | bytes 613120 | tf_op jit(solution)/shard_map/pallas_call | solution.py:30
  2.4 15.7 %all-to-all-start = ((bf16[16,4,896]{2,1,0:T(4,128)(2,1)}), bf16[16,4,896]{2,1,0:T(4,128)(2,1)S(1)}, u32[]{:S(2)}, u32[]{:S(2)}) async-start(bf16[16,4,896]{2,1,0:T(4,128)(2,1)} %get-tuple-element.26), calls=%async_computation | async-start | bytes 229376 | tf_op jit(solution)/shard_map/all_to_all | solution.py:175
  18.1 3.4 %collective-permute-start = (bf16[2,16,256]{2,1,0:T(8,128)(2,1)}, bf16[2,16,256]{2,1,0:T(8,128)(2,1)S(1)}, u32[]{:S(2)}, u32[]{:S(2)}) collective-permute-start(bf16[2,16,256]{2,1,0:T(8,128)(2,1)} %get-tuple-element.19), channel_id=1, source_target_pairs={{0,1},{1,2},{2,3},{3,4},{4,5},{5,6},{6,7},{7,8},{8,9},{9,10},{10,1... | collective-permute-start | bytes 49160 | tf_op jit(solution)/shard_map/ppermute | solution.py:196
  21.5 6.4 %collective-permute-start.1 = (bf16[2,16,256]{2,1,0:T(8,128)(2,1)}, bf16[2,16,256]{2,1,0:T(8,128)(2,1)S(1)}, u32[]{:S(2)}, u32[]{:S(2)}) collective-permute-start(bf16[2,16,256]{2,1,0:T(8,128)(2,1)} %get-tuple-element.20), channel_id=1, source_target_pairs={{1,0},{2,1},{3,2},{4,3},{5,4},{6,5},{7,6},{8,7},{9,8},{10,9},{11,1... | collective-permute-start | bytes 49160 | tf_op jit(solution)/shard_map/ppermute | solution.py:197
  27.8 0.0 collective-permute-done.above_ref
  27.9 4.3 %collective-permute-done.1.below_ref = bf16[2,16,256]{2,1,0:T(8,128)(2,1)S(1)} collective-permute-done((bf16[2,16,256]{2,1,0:T(8,128)(2,1)}, bf16[2,16,256]{2,1,0:T(8,128)(2,1)S(1)}, u32[]{:S(2)}, u32[]{:S(2)}) %collective-permute-start.1) | collective-permute-done | bytes 16416 | tf_op jit(solution)/shard_map/ppermute | solution.py:197
  32.1 1.0 %copy-done.1 = bf16[4,320,128]{2,1,0:T(8,128)(2,1)S(1)} copy-done((bf16[4,320,128]{2,1,0:T(8,128)(2,1)S(1)}, bf16[4,320,128]{2,1,0:T(8,128)(2,1)}, u32[]{:S(2)}) %copy-start.1) | copy-done | bytes 327704
  33.1 0.1 shard_map.51
  33.2 3.3 %collective-permute-start.2 = (bf16[352,128]{1,0:T(8,128)(2,1)S(1)}, bf16[352,128]{1,0:T(8,128)(2,1)S(1)}, u32[]{:S(2)}, u32[]{:S(2)}) collective-permute-start(bf16[352,128]{1,0:T(8,128)(2,1)S(1)} %get-tuple-element.22), channel_id=1, source_target_pairs={{0,128},{64,192},{128,0},{192,64},{256,384},{320,448},{384,256},{4... | collective-permute-start | bytes 270344 | tf_op jit(solution)/shard_map/ppermute | solution.py:163
  36.4 4.0 %collective-permute-start.3 = (bf16[352,128]{1,0:T(8,128)(2,1)S(1)}, bf16[352,128]{1,0:T(8,128)(2,1)S(1)}, u32[]{:S(2)}, u32[]{:S(2)}) collective-permute-start(bf16[352,128]{1,0:T(8,128)(2,1)S(1)} %get-tuple-element.23), channel_id=1, source_target_pairs={{0,256},{64,320},{128,384},{192,448},{256,0},{320,64},{384,128},{4... | collective-permute-start | bytes 270344 | tf_op jit(solution)/shard_map/ppermute | solution.py:163
  40.5 2.8 %collective-permute-start.4 = (bf16[352,128]{1,0:T(8,128)(2,1)S(1)}, bf16[352,128]{1,0:T(8,128)(2,1)S(1)}, u32[]{:S(2)}, u32[]{:S(2)}) collective-permute-start(bf16[352,128]{1,0:T(8,128)(2,1)S(1)} %get-tuple-element.24), channel_id=1, source_target_pairs={{0,384},{64,448},{128,256},{192,320},{256,128},{320,192},{384,0},{... | collective-permute-start | bytes 270344 | tf_op jit(solution)/shard_map/ppermute | solution.py:163
  43.3 0.0 all-to-all-done
  43.3 0.9 broadcast_in_dim.2
  44.2 4.8 %all-to-all-start.1 = ((bf16[4,16,4,896]{3,2,1,0:T(4,128)(2,1)}), bf16[4,16,4,896]{3,2,1,0:T(4,128)(2,1)S(1)}, u32[]{:S(2)}, u32[]{:S(2)}) async-start(bf16[4,16,4,896]{3,2,1,0:T(4,128)(2,1)} %broadcast_in_dim.2), calls=%async_computation.1 | async-start | bytes 917504 | tf_op jit(solution)/shard_map/all_to_all | solution.py:175
  49.0 0.0 collective-permute-done.2
  49.0 0.0 collective-permute-done.3
  49.0 2.3 %all-gather = bf16[8,352,128]{2,1,0:T(8,128)(2,1)S(1)} all-gather(bf16[4,352,128]{2,1,0:T(8,128)(2,1)S(1)} %pad_maximum_fusion), channel_id=2, replica_groups={{0,64},{128,192},{256,320},{384,448},{1,65},{129,193},{257,321},{385,44..., dimensions={0}, use_global_device_ids=true | all-gather | bytes 1081344 | tf_op jit(solution)/shard_map/all_gather | solution.py:211
  51.4 1.5 %shard_map.52 = (bf16[64,4,896]{2,1,0:T(4,128)(2,1)S(1)}, bf16[1024,1152]{1,0:T(8,128)(2,1)S(1)}) custom-call(bf16[2,4,352,128]{3,2,1,0:T(8,128)(2,1)S(1)} %bitcast.7), custom_call_target="tpu_custom_call" | custom-call | flops 603979776 | bytes 3538944 | tf_op jit(solution)/shard_map/pallas_call | solution.py:30
  52.9 0.8 copy-done
  53.7 0.9 %all-to-all-done.1 = bf16[4,16,4,896]{3,2,1,0:T(4,128)(2,1)S(1)} async-done(((bf16[4,16,4,896]{3,2,1,0:T(4,128)(2,1)}), bf16[4,16,4,896]{3,2,1,0:T(4,128)(2,1)S(1)}, u32[]{:S(2)}, u32[]{:S(2)}) %all-to-all-start.1) | async-done | bytes 458784 | tf_op jit(solution)/shard_map/all_to_all | solution.py:175
  54.6 15.2 %all-to-all-start.2 = ((bf16[64,4,896]{2,1,0:T(4,128)(2,1)}), bf16[64,4,896]{2,1,0:T(4,128)(2,1)S(1)}, u32[]{:S(2)}, u32[]{:S(2)}) async-start(bf16[64,4,896]{2,1,0:T(4,128)(2,1)} %copy-done), calls=%async_computation.2 | async-start | bytes 917504 | tf_op jit(solution)/shard_map/all_to_all | solution.py:175
  69.9 1.1 %shard_map.53 = (f32[4,128,256]{2,1,0:T(8,128)S(1)}, bf16[4,128,256]{2,1,0:T(8,128)(2,1)S(1)}) custom-call(bf16[1024,1152]{1,0:T(8,128)(2,1)S(1)} %get-tuple-element.25.windows_ref, bf16[64,4,896]{2,1,0:T(4,128)(2,1)S(1)} %bitcast.6), custom_call_target="tpu_custom_call" | custom-call | flops 603979776 | bytes 3604480 | tf_op jit(solution)/shard_map/pallas_call | solution.py:30
  71.0 1.9 %collective-permute-start.5 = (bf16[4,128,256]{2,1,0:T(8,128)(2,1)S(1)}, bf16[4,128,256]{2,1,0:T(8,128)(2,1)S(1)}, u32[]{:S(2)}, u32[]{:S(2)}) collective-permute-start(bf16[4,128,256]{2,1,0:T(8,128)(2,1)S(1)} %get-tuple-element.28), channel_id=1, source_target_pairs={{0,64},{64,0},{128,192},{192,128},{256,320},{320,256},{384,448},{4... | collective-permute-start | bytes 786440 | tf_op jit(solution)/shard_map/ppermute | solution.py:163
  72.9 1.5 %collective-permute-done.5.given_ref = bf16[4,128,256]{2,1,0:T(8,128)(2,1)S(1)} collective-permute-done((bf16[4,128,256]{2,1,0:T(8,128)(2,1)S(1)}, bf16[4,128,256]{2,1,0:T(8,128)(2,1)S(1)}, u32[]{:S(2)}, u32[]{:S(2)}) %collective-permute-start.5) | collective-permute-done | bytes 262176 | tf_op jit(solution)/shard_map/ppermute | solution.py:163
  74.4 2.4 %collective-permute-start.6 = (bf16[128,256]{1,0:T(8,128)(2,1)S(1)}, bf16[128,256]{1,0:T(8,128)(2,1)S(1)}, u32[]{:S(2)}, u32[]{:S(2)}) collective-permute-start(bf16[128,256]{1,0:T(8,128)(2,1)S(1)} %get-tuple-element.30), channel_id=1, source_target_pairs={{0,128},{64,192},{128,0},{192,64},{256,384},{320,448},{384,256},{4... | collective-permute-start | bytes 196616 | tf_op jit(solution)/shard_map/ppermute | solution.py:163
  76.8 4.9 %collective-permute-start.7 = (bf16[128,256]{1,0:T(8,128)(2,1)S(1)}, bf16[128,256]{1,0:T(8,128)(2,1)S(1)}, u32[]{:S(2)}, u32[]{:S(2)}) collective-permute-start(bf16[128,256]{1,0:T(8,128)(2,1)S(1)} %get-tuple-element.31), channel_id=1, source_target_pairs={{0,256},{64,320},{128,384},{192,448},{256,0},{320,64},{384,128},{4... | collective-permute-start | bytes 196616 | tf_op jit(solution)/shard_map/ppermute | solution.py:163
  81.8 2.8 %collective-permute-start.8 = (bf16[128,256]{1,0:T(8,128)(2,1)S(1)}, bf16[128,256]{1,0:T(8,128)(2,1)S(1)}, u32[]{:S(2)}, u32[]{:S(2)}) collective-permute-start(bf16[128,256]{1,0:T(8,128)(2,1)S(1)} %get-tuple-element.32), channel_id=1, source_target_pairs={{0,384},{64,448},{128,256},{192,320},{256,128},{320,192},{384,0},{... | collective-permute-start | bytes 196616 | tf_op jit(solution)/shard_map/ppermute | solution.py:163
  84.6 0.7 collective-permute-done.7.second_ref
  85.3 4.5 %collective-permute-done.8.third_ref = bf16[128,256]{1,0:T(8,128)(2,1)S(1)} collective-permute-done((bf16[128,256]{1,0:T(8,128)(2,1)S(1)}, bf16[128,256]{1,0:T(8,128)(2,1)S(1)}, u32[]{:S(2)}, u32[]{:S(2)}) %collective-permute-start.8) | collective-permute-done | bytes 65568 | tf_op jit(solution)/shard_map/ppermute | solution.py:163
  89.7 0.7 shard_map.55
  90.4 0.0 all-to-all-done.2.terms_ref
  90.4 0.9 shard_map.56
  (10 shorter events, 0.1 us)
Async XLA Ops:
  2.4 40.9 %all-to-all-start = ((bf16[16,4,896]{2,1,0:T(4,128)(2,1)}), bf16[16,4,896]{2,1,0:T(4,128)(2,1)S(1)}, u32[]{:S(2)}, u32[]{:S(2)}) async-start(bf16[16,4,896]{2,1,0:T(4,128)(2,1)} %get-tuple-element.26), calls=%async_computation | async-start | bytes 229376 | tf_op jit(solution)/shard_map/all_to_all | solution.py:175
  18.1 9.8 %collective-permute-start = (bf16[2,16,256]{2,1,0:T(8,128)(2,1)}, bf16[2,16,256]{2,1,0:T(8,128)(2,1)S(1)}, u32[]{:S(2)}, u32[]{:S(2)}) collective-permute-start(bf16[2,16,256]{2,1,0:T(8,128)(2,1)} %get-tuple-element.19), channel_id=1, source_target_pairs={{0,1},{1,2},{2,3},{3,4},{4,5},{5,6},{6,7},{7,8},{8,9},{9,10},{10,1... | collective-permute-start | bytes 49160 | tf_op jit(solution)/shard_map/ppermute | solution.py:196
  21.5 10.6 %collective-permute-start.1 = (bf16[2,16,256]{2,1,0:T(8,128)(2,1)}, bf16[2,16,256]{2,1,0:T(8,128)(2,1)S(1)}, u32[]{:S(2)}, u32[]{:S(2)}) collective-permute-start(bf16[2,16,256]{2,1,0:T(8,128)(2,1)} %get-tuple-element.20), channel_id=1, source_target_pairs={{1,0},{2,1},{3,2},{4,3},{5,4},{6,5},{7,6},{8,7},{9,8},{10,9},{11,1... | collective-permute-start | bytes 49160 | tf_op jit(solution)/shard_map/ppermute | solution.py:197
  32.1 1.0 %copy-start.1 = (bf16[4,320,128]{2,1,0:T(8,128)(2,1)S(1)}, bf16[4,320,128]{2,1,0:T(8,128)(2,1)}, u32[]{:S(2)}) copy-start(bf16[4,320,128]{2,1,0:T(8,128)(2,1)} %get-tuple-element.18.body_ref) | copy-start | bytes 983044
  33.2 15.8 %collective-permute-start.2 = (bf16[352,128]{1,0:T(8,128)(2,1)S(1)}, bf16[352,128]{1,0:T(8,128)(2,1)S(1)}, u32[]{:S(2)}, u32[]{:S(2)}) collective-permute-start(bf16[352,128]{1,0:T(8,128)(2,1)S(1)} %get-tuple-element.22), channel_id=1, source_target_pairs={{0,128},{64,192},{128,0},{192,64},{256,384},{320,448},{384,256},{4... | collective-permute-start | bytes 270344 | tf_op jit(solution)/shard_map/ppermute | solution.py:163
  36.4 12.5 %collective-permute-start.3 = (bf16[352,128]{1,0:T(8,128)(2,1)S(1)}, bf16[352,128]{1,0:T(8,128)(2,1)S(1)}, u32[]{:S(2)}, u32[]{:S(2)}) collective-permute-start(bf16[352,128]{1,0:T(8,128)(2,1)S(1)} %get-tuple-element.23), channel_id=1, source_target_pairs={{0,256},{64,320},{128,384},{192,448},{256,0},{320,64},{384,128},{4... | collective-permute-start | bytes 270344 | tf_op jit(solution)/shard_map/ppermute | solution.py:163
  40.5 8.5 %collective-permute-start.4 = (bf16[352,128]{1,0:T(8,128)(2,1)S(1)}, bf16[352,128]{1,0:T(8,128)(2,1)S(1)}, u32[]{:S(2)}, u32[]{:S(2)}) collective-permute-start(bf16[352,128]{1,0:T(8,128)(2,1)S(1)} %get-tuple-element.24), channel_id=1, source_target_pairs={{0,384},{64,448},{128,256},{192,320},{256,128},{320,192},{384,0},{... | collective-permute-start | bytes 270344 | tf_op jit(solution)/shard_map/ppermute | solution.py:163
  44.2 10.4 %all-to-all-start.1 = ((bf16[4,16,4,896]{3,2,1,0:T(4,128)(2,1)}), bf16[4,16,4,896]{3,2,1,0:T(4,128)(2,1)S(1)}, u32[]{:S(2)}, u32[]{:S(2)}) async-start(bf16[4,16,4,896]{3,2,1,0:T(4,128)(2,1)} %broadcast_in_dim.2), calls=%async_computation.1 | async-start | bytes 917504 | tf_op jit(solution)/shard_map/all_to_all | solution.py:175
  52.9 0.8 copy-start
  53.7 36.0 %copy-start.2 = (bf16[2,4,16,256]{3,2,1,0:T(8,128)(2,1)S(1)}, bf16[2,4,16,256]{3,2,1,0:T(8,128)(2,1)}, u32[]{:S(2)}) copy-start(bf16[2,4,16,256]{3,2,1,0:T(8,128)(2,1)} %inputs_ref.3) | copy-start | bytes 196612
  53.7 36.0 %copy-start.3 = (bf16[2,4,16,256]{3,2,1,0:T(8,128)(2,1)S(1)}, bf16[2,4,16,256]{3,2,1,0:T(8,128)(2,1)}, u32[]{:S(2)}) copy-start(bf16[2,4,16,256]{3,2,1,0:T(8,128)(2,1)} %cot_ref.3) | copy-start | bytes 196612
  54.6 35.8 %all-to-all-start.2 = ((bf16[64,4,896]{2,1,0:T(4,128)(2,1)}), bf16[64,4,896]{2,1,0:T(4,128)(2,1)S(1)}, u32[]{:S(2)}, u32[]{:S(2)}) async-start(bf16[64,4,896]{2,1,0:T(4,128)(2,1)} %copy-done), calls=%async_computation.2 | async-start | bytes 917504 | tf_op jit(solution)/shard_map/all_to_all | solution.py:175
  71.0 3.4 %collective-permute-start.5 = (bf16[4,128,256]{2,1,0:T(8,128)(2,1)S(1)}, bf16[4,128,256]{2,1,0:T(8,128)(2,1)S(1)}, u32[]{:S(2)}, u32[]{:S(2)}) collective-permute-start(bf16[4,128,256]{2,1,0:T(8,128)(2,1)S(1)} %get-tuple-element.28), channel_id=1, source_target_pairs={{0,64},{64,0},{128,192},{192,128},{256,320},{320,256},{384,448},{4... | collective-permute-start | bytes 786440 | tf_op jit(solution)/shard_map/ppermute | solution.py:163
  74.4 10.1 %collective-permute-start.6 = (bf16[128,256]{1,0:T(8,128)(2,1)S(1)}, bf16[128,256]{1,0:T(8,128)(2,1)S(1)}, u32[]{:S(2)}, u32[]{:S(2)}) collective-permute-start(bf16[128,256]{1,0:T(8,128)(2,1)S(1)} %get-tuple-element.30), channel_id=1, source_target_pairs={{0,128},{64,192},{128,0},{192,64},{256,384},{320,448},{384,256},{4... | collective-permute-start | bytes 196616 | tf_op jit(solution)/shard_map/ppermute | solution.py:163
  76.8 8.5 %collective-permute-start.7 = (bf16[128,256]{1,0:T(8,128)(2,1)S(1)}, bf16[128,256]{1,0:T(8,128)(2,1)S(1)}, u32[]{:S(2)}, u32[]{:S(2)}) collective-permute-start(bf16[128,256]{1,0:T(8,128)(2,1)S(1)} %get-tuple-element.31), channel_id=1, source_target_pairs={{0,256},{64,320},{128,384},{192,448},{256,0},{320,64},{384,128},{4... | collective-permute-start | bytes 196616 | tf_op jit(solution)/shard_map/ppermute | solution.py:163
  81.8 8.0 %collective-permute-start.8 = (bf16[128,256]{1,0:T(8,128)(2,1)S(1)}, bf16[128,256]{1,0:T(8,128)(2,1)S(1)}, u32[]{:S(2)}, u32[]{:S(2)}) collective-permute-start(bf16[128,256]{1,0:T(8,128)(2,1)S(1)} %get-tuple-element.32), channel_id=1, source_target_pairs={{0,384},{64,448},{128,256},{192,320},{256,128},{320,192},{384,0},{... | collective-permute-start | bytes 196616 | tf_op jit(solution)/shard_map/ppermute | solution.py:163

commit v3 on v2

--- a/solution.py
+++ b/solution.py
@@ -11,6 +11,7 @@
 CHIPS = 4
 CORES = 2
 GROUPS = CHIPS * CORES
+PAIRS = [[CORES * chip + core for core in range(CORES)] for chip in range(CHIPS)]
 FAR = 4
 OWN = 32
 TAPS = 27
@@ -42,27 +43,50 @@
     return jax.ShapeDtypeStruct(shape, dtype)
 
 
-def prepare(kernel_ref, inputs_ref, cot_ref, blocks_ref, above_ref, below_ref, body_ref):
+def prepare(kernel_ref, inputs_ref, cot_ref, swap_ref, second_ref, body_ref):
     own_in = kernel_ref.shape[1]
-    _, channels = inputs_ref.shape[2:]
-    above_ref[...] = cot_ref[:, cot_ref.shape[1] - 1]
-    below_ref[...] = cot_ref[:, 0]
+    across, channels = inputs_ref.shape[2:]
+    odd = lax.axis_index("rows") % 2
+    last = cot_ref.shape[1] - 1
+    for ref, row in ((swap_ref, (1 - odd) * last), (second_ref, odd * last)):
+        for frame in range(2):
+            values = cot_ref[frame, row]
+            for tile in range(2):
+                start = across * (2 * frame + tile)
+                ref[start : start + across] = values[:, LANES * tile : LANES * tile + LANES]
+    pieces = [kernel_ref[tap].astype(F32) for tap in range(TAPS)]
+    pieces.append(jnp.zeros((own_in, SLOT - TAPS * OWN), F32))
+    slot = jnp.concatenate(pieces, axis=1)
+    tiles = [slot[:, start : start + LANES] for start in range(0, SLOT, LANES)]
+    tiles.append(jnp.zeros((swap_ref.shape[0] - 4 * across - SLOT // LANES * own_in, LANES), F32))
+    swap_ref[4 * across :] = jnp.concatenate(tiles, axis=0).astype(BF16)
     body_ref[:, :channels] = jnp.broadcast_to(
         jax.nn.silu(inputs_ref[...].reshape(-1, channels).astype(F32)).T.astype(BF16)[None],
         (CHIPS, channels, LANES),
     )
     halves = [cot_ref[frame].reshape(-1, channels).astype(F32) for frame in range(2)]
     for target in range(CHIPS):
-        body_ref[target, channels:] = for_chip(target, *halves)
-    pieces = [kernel_ref[tap].astype(F32) for tap in range(TAPS)]
-    pieces.append(jnp.zeros((own_in, SLOT - TAPS * OWN), F32))
-    slot = jnp.concatenate(pieces, axis=1).astype(BF16)
-    blocks_ref[...] = jnp.broadcast_to(slot[None], blocks_ref.shape)
+        body_ref[target, channels:] = for_chip(target, halves[0], halves[1])
+
+
+def joined(own_ref, swapped_ref, blocks_ref):
+    own_in = blocks_ref.shape[2]
+    start = own_ref.shape[0] - LANES // 4
+    odd = lax.axis_index("rows") % 2
+    for place, ref in ((odd, own_ref), (1 - odd, swapped_ref)):
+        values = ref[start:].astype(F32)
+        tiles = [values[own_in * tile : own_in * tile + own_in] for tile in range(SLOT // LANES)]
+        slot = jnp.concatenate(tiles, axis=1).astype(BF16)
+        for pair in range(blocks_ref.shape[0]):
+            blocks_ref[pair, place] = slot
 
 
 def for_chip(target, first, second):
     tile = slice(LANES * (target // 2), LANES * (target // 2) + LANES)
-    first, second = first[:, tile], second[:, tile]
+    return halved(target, first[:, tile], second[:, tile])
+
+
+def halved(target, first, second):
     low = lax.broadcasted_iota(jnp.int32, first.shape, 1) < LANES // 2
     if target % 2 == 0:
         second = pltpu.roll(second, LANES // 2, 1)
@@ -71,15 +95,18 @@
     return jnp.where(low, first, second).astype(BF16)
 
 
-def pack(body_ref, above_ref, below_ref, *out_and_scratch):
+def pack(body_ref, first_ref, second_ref, *out_and_scratch):
     outs, halo = out_and_scratch[:CHIPS], out_and_scratch[CHIPS]
     chip, _ = chip_and_core()
     rows = body_ref.shape[1]
-    across = above_ref.shape[1]
-    for side, ref in enumerate((above_ref, below_ref)):
-        halves = [ref[frame].astype(F32) for frame in range(2)]
+    across = 16
+    odd = lax.axis_index("rows") % 2
+    for side, ref in ((1 - odd, first_ref), (odd, second_ref)):
+        tiles = [ref[across * tile : across * tile + across].astype(F32) for tile in range(4)]
         for target in range(CHIPS):
-            halo[target, across * side : across * side + across] = for_chip(target, *halves)
+            tile = target // 2
+            part = halved(target, tiles[tile], tiles[2 + tile])
+            halo[target, pl.ds(pl.multiple_of(across * side, across), across)] = part
     for step, out in enumerate(outs):
         out[:rows] = body_ref[chip ^ step]
         out[rows:] = halo[chip ^ step]
@@ -166,7 +193,7 @@
 def near_and_far(bands):
     near = bands // FAR
     return (
-        [[near * x + i for i in range(near)] for x in range(FAR)],
+        [[near * x + 2 * i + odd for i in range(near // 2)] for x in range(FAR) for odd in range(2)],
         [[near * x + i for x in range(FAR)] for i in range(near)],
     )
 
@@ -184,31 +211,35 @@
     points = frames * height * across
 
     held = height * across
-    blocks, above, below, body = called(
+    swap, second, body = called(
         prepare,
         [
-            array((bands // FAR, own_in, SLOT)), array((frames, across, channels)),
-            array((frames, across, channels)), array((CHIPS, channels + held, LANES)),
+            array((4 * across + LANES // 4, LANES)), array((4 * across, LANES)),
+            array((CHIPS, channels + held, LANES)),
         ],
         kernel, inputs, cotangent, limit=60,
     )
-    forward = [(i, i + 1) for i in range(bands - 1)]
-    above = lax.ppermute(above, "rows", forward)
-    below = lax.ppermute(below, "rows", [(b, a) for a, b in forward])
+    first = lax.ppermute(swap, "rows", [(i, i ^ 1) for i in range(bands)])
+    pairs = [(i, i + 1) for i in range(1, bands - 1, 2)]
+    second = lax.ppermute(second, "rows", pairs + [(b, a) for a, b in pairs])
+    blocks, = called(joined, [array((bands // FAR // 2, 2, own_in, SLOT))], swap, first)
 
     near, far = near_and_far(bands)
     blocks = exchanged(blocks, near)
+    blocks = blocks.reshape(bands // FAR, own_in, SLOT)
     blocks = jnp.broadcast_to(blocks[None], (FAR, *blocks.shape))
     kernel_in = exchanged(blocks, far).reshape(bands, own_in, SLOT)
 
     span = (height + 2) * across
     payload = array((channels + span, LANES))
     packs = called(
-        pack, [payload] * CHIPS, body, above, below,
+        pack, [payload] * CHIPS, body, first, second,
         scratch=[pltpu.VMEM((CHIPS, 2 * across, LANES), BF16)],
     )
     packs = [packs[0]] + [stepped(packs[step], CORES * step) for step in range(1, CHIPS)]
-    every = lax.all_gather(jnp.stack(packs), "tm", axis=0, axis_index_groups=[[2 * i, 2 * i + 1] for i in range(CHIPS)])
+    every = lax.all_gather(
+        jnp.stack(packs), "tm", axis=0, axis_index_groups=PAIRS
+    )
 
     factor = float(points * GROUPS * bands) ** (-0.5)
 

time: 92 us -> 94.8 us (1.030)
  waiting for transfers between devices: 11.8 us -> 17.3 us
  starting transfers between devices: 67.6 us -> 63.5 us
    ppermute x2, waiting for transfers between devices: 4.26 us -> 9.66 us  [the longest x1 5.15 us: local(): first = lax.ppermute(swap, 'rows', [(i, i ^ 1) for i in range(bands)])]
    all_to_all x3, starting transfers between devices: 35.7 us -> 30.5 us  [exchanged(): lax.all_to_all(blocks, 'rows', split_axis=0, concat_axis=0, tiled=True, a...]
    ppermute x2, starting transfers between devices: 9.74 us -> 10.8 us  [the longest x1 6.12 us: local(): second = lax.ppermute(second, 'rows', pairs + [(b, a) for a, b in pairs])]
    unnamed x8 -> x10, local copies, waits for them, and re-layouts: 1.75 us -> 2.49 us
    pallas_call x7 -> x8, Pallas kernels: 6.14 us -> 6.8 us  [called(): pl.pallas_call(body, out_shape=outs, in_specs=[whole] * len(args), out_sp...]
  transfers between devices with their start and end apart: 12 -> 12, of which waited for: 5 -> 6; matrix products, arithmetic and copies ran while one was open for 1% -> 1% of each run, Pallas kernels for 4% -> 4%
where the time goes in v3:
time: 94.8 us; the launch traced here: 94.1 us
  starting transfers between devices  63.5 us (67%)
  waiting for transfers between devices  17.3 us (18%)
  Pallas kernels  6.8 us (7%)
  local copies, waits for them, and re-layouts  3.38 us (4%)
  blocking collectives  2.32 us (2%)
    all_to_all x3, starting transfers between devices, exchanged(): lax.all_to_all(blocks, 'rows', split_axis=0, concat_axis=0, tiled=True, a...  30.5 us
    ppermute x7, starting transfers between devices, stepped(): return lax.ppermute(block, 'tm', [(i, i ^ step) for i in range(count)])  22.1 us
    pallas_call x8, Pallas kernels, called(): pl.pallas_call(body, out_shape=outs, in_specs=[whole] * len(args), out_sp...  6.8 us
    ppermute x7, waiting for transfers between devices, stepped(): return lax.ppermute(block, 'tm', [(i, i ^ step) for i in range(count)])  6.67 us
    ppermute x1, starting transfers between devices, local(): second = lax.ppermute(second, 'rows', pairs + [(b, a) for a, b in pairs])  6.12 us
    ppermute x1, waiting for transfers between devices, local(): first = lax.ppermute(swap, 'rows', [(i, i ^ 1) for i in range(bands)])  5.15 us
    ppermute x1, starting transfers between devices, local(): first = lax.ppermute(swap, 'rows', [(i, i ^ 1) for i in range(bands)])  4.7 us
    ppermute x1, waiting for transfers between devices, local(): second = lax.ppermute(second, 'rows', pairs + [(b, a) for a, b in pairs])  4.51 us
  transfers between devices with their start and end apart: 12, of which 6 were waited for; matrix products, arithmetic and copies ran while one was open for 1% of the time, Pallas kernels for 4%

profile of v3, /device:TPU:62, one launch (start us, length us, event | category | flops | bytes accessed | tf_op | source)
XLA Modules:
  0.0 94.1 jit_solution(10897459273507071430)
XLA Ops:
  0.6 1.8 %shard_map.50 = (bf16[96,128]{1,0:T(8,128)(2,1)}, bf16[64,128]{1,0:T(8,128)(2,1)}, bf16[4,320,128]{2,1,0:T(8,128)(2,1)}) custom-call(bf16[27,4,32]{2,1,0:T(4,128)(2,1)} %kernel_ref.1, bf16[2,4,16,256]{3,2,1,0:T(8,128)(2,1)} %inputs_ref.3, bf16[2,4,16,256]{3,2,1,0:T(8,128)(2,1)} %cot_ref.3), custom_call_target="tpu_custom_call" | custom-call | bytes 506624 | tf_op jit(solution)/shard_map/pallas_call | solution.py:31
  2.4 4.7 %collective-permute-start = (bf16[96,128]{1,0:T(8,128)(2,1)}, bf16[96,128]{1,0:T(8,128)(2,1)S(1)}, u32[]{:S(2)}, u32[]{:S(2)}) collective-permute-start(bf16[96,128]{1,0:T(8,128)(2,1)} %get-tuple-element.18.own_ref), channel_id=1, source_target_pairs={{0,1},{1,0},{2,3},{3,2},{4,5},{5,4},{6,7},{7,6},{8,9},{9,8},{10,11... | collective-permute-start | bytes 73736 | tf_op jit(solution)/shard_map/ppermute | solution.py:222
  7.1 5.2 %collective-permute-done.first_ref.swapped_ref = bf16[96,128]{1,0:T(8,128)(2,1)S(1)} collective-permute-done((bf16[96,128]{1,0:T(8,128)(2,1)}, bf16[96,128]{1,0:T(8,128)(2,1)S(1)}, u32[]{:S(2)}, u32[]{:S(2)}) %collective-permute-start) | collective-permute-done | bytes 24608 | tf_op jit(solution)/shard_map/ppermute | solution.py:222
  12.3 0.7 copy-done.4
  13.0 0.7 shard_map.53
  13.7 10.3 %all-to-all-start = ((bf16[8,2,4,896]{3,2,1,0:T(4,128)(2,1)}), bf16[8,2,4,896]{3,2,1,0:T(4,128)(2,1)S(1)}, u32[]{:S(2)}, u32[]{:S(2)}) async-start(bf16[8,2,4,896]{3,2,1,0:T(4,128)(2,1)} %shard_map.53), calls=%async_computation | async-start | bytes 229376 | tf_op jit(solution)/shard_map/all_to_all | solution.py:202
  24.0 6.1 %collective-permute-start.1 = (bf16[64,128]{1,0:T(8,128)(2,1)}, bf16[64,128]{1,0:T(8,128)(2,1)S(1)}, u32[]{:S(2)}, u32[]{:S(2)}) collective-permute-start(bf16[64,128]{1,0:T(8,128)(2,1)} %get-tuple-element.19), channel_id=1, source_target_pairs={{1,2},{3,4},{5,6},{7,8},{9,10},{11,12},{13,14},{15,16},{17,18},{19... | collective-permute-start | bytes 49160 | tf_op jit(solution)/shard_map/ppermute | solution.py:224
  30.1 4.5 %collective-permute-done.1.second_ref = bf16[64,128]{1,0:T(8,128)(2,1)S(1)} collective-permute-done((bf16[64,128]{1,0:T(8,128)(2,1)}, bf16[64,128]{1,0:T(8,128)(2,1)S(1)}, u32[]{:S(2)}, u32[]{:S(2)}) %collective-permute-start.1) | collective-permute-done | bytes 16416 | tf_op jit(solution)/shard_map/ppermute | solution.py:224
  34.6 1.0 %copy-done.1 = bf16[4,320,128]{2,1,0:T(8,128)(2,1)S(1)} copy-done((bf16[4,320,128]{2,1,0:T(8,128)(2,1)S(1)}, bf16[4,320,128]{2,1,0:T(8,128)(2,1)}, u32[]{:S(2)}) %copy-start.1) | copy-done | bytes 327704
  35.6 0.1 shard_map.51
  35.7 3.2 %collective-permute-start.2 = (bf16[352,128]{1,0:T(8,128)(2,1)S(1)}, bf16[352,128]{1,0:T(8,128)(2,1)S(1)}, u32[]{:S(2)}, u32[]{:S(2)}) collective-permute-start(bf16[352,128]{1,0:T(8,128)(2,1)S(1)} %get-tuple-element.21), channel_id=1, source_target_pairs={{0,128},{64,192},{128,0},{192,64},{256,384},{320,448},{384,256},{4... | collective-permute-start | bytes 270344 | tf_op jit(solution)/shard_map/ppermute | solution.py:190
  38.9 4.1 %collective-permute-start.3 = (bf16[352,128]{1,0:T(8,128)(2,1)S(1)}, bf16[352,128]{1,0:T(8,128)(2,1)S(1)}, u32[]{:S(2)}, u32[]{:S(2)}) collective-permute-start(bf16[352,128]{1,0:T(8,128)(2,1)S(1)} %get-tuple-element.22), channel_id=1, source_target_pairs={{0,256},{64,320},{128,384},{192,448},{256,0},{320,64},{384,128},{4... | collective-permute-start | bytes 270344 | tf_op jit(solution)/shard_map/ppermute | solution.py:190
  43.0 2.8 %collective-permute-start.4 = (bf16[352,128]{1,0:T(8,128)(2,1)S(1)}, bf16[352,128]{1,0:T(8,128)(2,1)S(1)}, u32[]{:S(2)}, u32[]{:S(2)}) collective-permute-start(bf16[352,128]{1,0:T(8,128)(2,1)S(1)} %get-tuple-element.23), channel_id=1, source_target_pairs={{0,384},{64,448},{128,256},{192,320},{256,128},{320,192},{384,0},{... | collective-permute-start | bytes 270344 | tf_op jit(solution)/shard_map/ppermute | solution.py:190
  45.8 0.0 all-to-all-done
  45.8 0.9 broadcast_in_dim.8
  46.7 4.8 %all-to-all-start.1 = ((bf16[4,16,4,896]{3,2,1,0:T(4,128)(2,1)}), bf16[4,16,4,896]{3,2,1,0:T(4,128)(2,1)S(1)}, u32[]{:S(2)}, u32[]{:S(2)}) async-start(bf16[4,16,4,896]{3,2,1,0:T(4,128)(2,1)} %broadcast_in_dim.8), calls=%async_computation.1 | async-start | bytes 917504 | tf_op jit(solution)/shard_map/all_to_all | solution.py:202
  51.5 0.0 collective-permute-done.2
  51.5 2.3 %all-gather = bf16[8,352,128]{2,1,0:T(8,128)(2,1)S(1)} all-gather(bf16[4,352,128]{2,1,0:T(8,128)(2,1)S(1)} %pad_maximum_fusion), channel_id=2, replica_groups={{0,64},{128,192},{256,320},{384,448},{1,65},{129,193},{257,321},{385,44..., dimensions={0}, use_global_device_ids=true | all-gather | bytes 1081344 | tf_op jit(solution)/shard_map/all_gather | solution.py:240
  53.9 1.5 %shard_map.52 = (bf16[64,4,896]{2,1,0:T(4,128)(2,1)S(1)}, bf16[1024,1152]{1,0:T(8,128)(2,1)S(1)}) custom-call(bf16[2,4,352,128]{3,2,1,0:T(8,128)(2,1)S(1)} %bitcast.8), custom_call_target="tpu_custom_call" | custom-call | flops 603979776 | bytes 3538944 | tf_op jit(solution)/shard_map/pallas_call | solution.py:31
  55.4 0.8 copy-done
  56.2 0.9 %all-to-all-done.1 = bf16[4,16,4,896]{3,2,1,0:T(4,128)(2,1)S(1)} async-done(((bf16[4,16,4,896]{3,2,1,0:T(4,128)(2,1)}), bf16[4,16,4,896]{3,2,1,0:T(4,128)(2,1)S(1)}, u32[]{:S(2)}, u32[]{:S(2)}) %all-to-all-start.1) | async-done | bytes 458784 | tf_op jit(solution)/shard_map/all_to_all | solution.py:202
  57.1 15.5 %all-to-all-start.2 = ((bf16[64,4,896]{2,1,0:T(4,128)(2,1)}), bf16[64,4,896]{2,1,0:T(4,128)(2,1)S(1)}, u32[]{:S(2)}, u32[]{:S(2)}) async-start(bf16[64,4,896]{2,1,0:T(4,128)(2,1)} %copy-done), calls=%async_computation.2 | async-start | bytes 917504 | tf_op jit(solution)/shard_map/all_to_all | solution.py:202
  72.6 1.1 %shard_map.54 = (f32[4,128,256]{2,1,0:T(8,128)S(1)}, bf16[4,128,256]{2,1,0:T(8,128)(2,1)S(1)}) custom-call(bf16[1024,1152]{1,0:T(8,128)(2,1)S(1)} %get-tuple-element.24.windows_ref, bf16[64,4,896]{2,1,0:T(4,128)(2,1)S(1)} %bitcast.7), custom_call_target="tpu_custom_call" | custom-call | flops 603979776 | bytes 3604480 | tf_op jit(solution)/shard_map/pallas_call | solution.py:31
  73.7 1.9 %collective-permute-start.5 = (bf16[4,128,256]{2,1,0:T(8,128)(2,1)S(1)}, bf16[4,128,256]{2,1,0:T(8,128)(2,1)S(1)}, u32[]{:S(2)}, u32[]{:S(2)}) collective-permute-start(bf16[4,128,256]{2,1,0:T(8,128)(2,1)S(1)} %get-tuple-element.26), channel_id=1, source_target_pairs={{0,64},{64,0},{128,192},{192,128},{256,320},{320,256},{384,448},{4... | collective-permute-start | bytes 786440 | tf_op jit(solution)/shard_map/ppermute | solution.py:190
  75.6 1.5 %collective-permute-done.5.given_ref = bf16[4,128,256]{2,1,0:T(8,128)(2,1)S(1)} collective-permute-done((bf16[4,128,256]{2,1,0:T(8,128)(2,1)S(1)}, bf16[4,128,256]{2,1,0:T(8,128)(2,1)S(1)}, u32[]{:S(2)}, u32[]{:S(2)}) %collective-permute-start.5) | collective-permute-done | bytes 262176 | tf_op jit(solution)/shard_map/ppermute | solution.py:190
  77.2 2.3 %collective-permute-start.6 = (bf16[128,256]{1,0:T(8,128)(2,1)S(1)}, bf16[128,256]{1,0:T(8,128)(2,1)S(1)}, u32[]{:S(2)}, u32[]{:S(2)}) collective-permute-start(bf16[128,256]{1,0:T(8,128)(2,1)S(1)} %get-tuple-element.28), channel_id=1, source_target_pairs={{0,128},{64,192},{128,0},{192,64},{256,384},{320,448},{384,256},{4... | collective-permute-start | bytes 196616 | tf_op jit(solution)/shard_map/ppermute | solution.py:190
  79.5 5.0 %collective-permute-start.7 = (bf16[128,256]{1,0:T(8,128)(2,1)S(1)}, bf16[128,256]{1,0:T(8,128)(2,1)S(1)}, u32[]{:S(2)}, u32[]{:S(2)}) collective-permute-start(bf16[128,256]{1,0:T(8,128)(2,1)S(1)} %get-tuple-element.29), channel_id=1, source_target_pairs={{0,256},{64,320},{128,384},{192,448},{256,0},{320,64},{384,128},{4... | collective-permute-start | bytes 196616 | tf_op jit(solution)/shard_map/ppermute | solution.py:190
  84.5 2.8 %collective-permute-start.8 = (bf16[128,256]{1,0:T(8,128)(2,1)S(1)}, bf16[128,256]{1,0:T(8,128)(2,1)S(1)}, u32[]{:S(2)}, u32[]{:S(2)}) collective-permute-start(bf16[128,256]{1,0:T(8,128)(2,1)S(1)} %get-tuple-element.30), channel_id=1, source_target_pairs={{0,384},{64,448},{128,256},{192,320},{256,128},{320,192},{384,0},{... | collective-permute-start | bytes 196616 | tf_op jit(solution)/shard_map/ppermute | solution.py:190
  87.3 0.7 collective-permute-done.7.second_ref
  88.0 4.5 %collective-permute-done.8.third_ref = bf16[128,256]{1,0:T(8,128)(2,1)S(1)} collective-permute-done((bf16[128,256]{1,0:T(8,128)(2,1)S(1)}, bf16[128,256]{1,0:T(8,128)(2,1)S(1)}, u32[]{:S(2)}, u32[]{:S(2)}) %collective-permute-start.8) | collective-permute-done | bytes 65568 | tf_op jit(solution)/shard_map/ppermute | solution.py:190
  92.5 0.7 shard_map.56
  93.2 0.9 shard_map.57
  (13 shorter events, 0.1 us)
Async XLA Ops:
  2.4 9.9 %collective-permute-start = (bf16[96,128]{1,0:T(8,128)(2,1)}, bf16[96,128]{1,0:T(8,128)(2,1)S(1)}, u32[]{:S(2)}, u32[]{:S(2)}) collective-permute-start(bf16[96,128]{1,0:T(8,128)(2,1)} %get-tuple-element.18.own_ref), channel_id=1, source_target_pairs={{0,1},{1,0},{2,3},{3,2},{4,5},{5,4},{6,7},{7,6},{8,9},{9,8},{10,11... | collective-permute-start | bytes 73736 | tf_op jit(solution)/shard_map/ppermute | solution.py:222
  12.3 0.7 copy-start.4
  13.7 32.2 %all-to-all-start = ((bf16[8,2,4,896]{3,2,1,0:T(4,128)(2,1)}), bf16[8,2,4,896]{3,2,1,0:T(4,128)(2,1)S(1)}, u32[]{:S(2)}, u32[]{:S(2)}) async-start(bf16[8,2,4,896]{3,2,1,0:T(4,128)(2,1)} %shard_map.53), calls=%async_computation | async-start | bytes 229376 | tf_op jit(solution)/shard_map/all_to_all | solution.py:202
  24.0 10.6 %collective-permute-start.1 = (bf16[64,128]{1,0:T(8,128)(2,1)}, bf16[64,128]{1,0:T(8,128)(2,1)S(1)}, u32[]{:S(2)}, u32[]{:S(2)}) collective-permute-start(bf16[64,128]{1,0:T(8,128)(2,1)} %get-tuple-element.19), channel_id=1, source_target_pairs={{1,2},{3,4},{5,6},{7,8},{9,10},{11,12},{13,14},{15,16},{17,18},{19... | collective-permute-start | bytes 49160 | tf_op jit(solution)/shard_map/ppermute | solution.py:224
  34.6 1.0 %copy-start.1 = (bf16[4,320,128]{2,1,0:T(8,128)(2,1)S(1)}, bf16[4,320,128]{2,1,0:T(8,128)(2,1)}, u32[]{:S(2)}) copy-start(bf16[4,320,128]{2,1,0:T(8,128)(2,1)} %get-tuple-element.17.body_ref) | copy-start | bytes 983044
  35.7 15.8 %collective-permute-start.2 = (bf16[352,128]{1,0:T(8,128)(2,1)S(1)}, bf16[352,128]{1,0:T(8,128)(2,1)S(1)}, u32[]{:S(2)}, u32[]{:S(2)}) collective-permute-start(bf16[352,128]{1,0:T(8,128)(2,1)S(1)} %get-tuple-element.21), channel_id=1, source_target_pairs={{0,128},{64,192},{128,0},{192,64},{256,384},{320,448},{384,256},{4... | collective-permute-start | bytes 270344 | tf_op jit(solution)/shard_map/ppermute | solution.py:190
  38.9 12.6 %collective-permute-start.3 = (bf16[352,128]{1,0:T(8,128)(2,1)S(1)}, bf16[352,128]{1,0:T(8,128)(2,1)S(1)}, u32[]{:S(2)}, u32[]{:S(2)}) collective-permute-start(bf16[352,128]{1,0:T(8,128)(2,1)S(1)} %get-tuple-element.22), channel_id=1, source_target_pairs={{0,256},{64,320},{128,384},{192,448},{256,0},{320,64},{384,128},{4... | collective-permute-start | bytes 270344 | tf_op jit(solution)/shard_map/ppermute | solution.py:190
  43.0 8.5 %collective-permute-start.4 = (bf16[352,128]{1,0:T(8,128)(2,1)S(1)}, bf16[352,128]{1,0:T(8,128)(2,1)S(1)}, u32[]{:S(2)}, u32[]{:S(2)}) collective-permute-start(bf16[352,128]{1,0:T(8,128)(2,1)S(1)} %get-tuple-element.23), channel_id=1, source_target_pairs={{0,384},{64,448},{128,256},{192,320},{256,128},{320,192},{384,0},{... | collective-permute-start | bytes 270344 | tf_op jit(solution)/shard_map/ppermute | solution.py:190
  46.7 10.4 %all-to-all-start.1 = ((bf16[4,16,4,896]{3,2,1,0:T(4,128)(2,1)}), bf16[4,16,4,896]{3,2,1,0:T(4,128)(2,1)S(1)}, u32[]{:S(2)}, u32[]{:S(2)}) async-start(bf16[4,16,4,896]{3,2,1,0:T(4,128)(2,1)} %broadcast_in_dim.8), calls=%async_computation.1 | async-start | bytes 917504 | tf_op jit(solution)/shard_map/all_to_all | solution.py:202
  55.4 0.8 copy-start
  56.2 36.3 %copy-start.2 = (bf16[2,4,16,256]{3,2,1,0:T(8,128)(2,1)S(1)}, bf16[2,4,16,256]{3,2,1,0:T(8,128)(2,1)}, u32[]{:S(2)}) copy-start(bf16[2,4,16,256]{3,2,1,0:T(8,128)(2,1)} %inputs_ref.3) | copy-start | bytes 196612
  56.2 36.3 %copy-start.3 = (bf16[2,4,16,256]{3,2,1,0:T(8,128)(2,1)S(1)}, bf16[2,4,16,256]{3,2,1,0:T(8,128)(2,1)}, u32[]{:S(2)}) copy-start(bf16[2,4,16,256]{3,2,1,0:T(8,128)(2,1)} %cot_ref.3) | copy-start | bytes 196612
  57.1 36.1 %all-to-all-start.2 = ((bf16[64,4,896]{2,1,0:T(4,128)(2,1)}), bf16[64,4,896]{2,1,0:T(4,128)(2,1)S(1)}, u32[]{:S(2)}, u32[]{:S(2)}) async-start(bf16[64,4,896]{2,1,0:T(4,128)(2,1)} %copy-done), calls=%async_computation.2 | async-start | bytes 917504 | tf_op jit(solution)/shard_map/all_to_all | solution.py:202
  73.7 3.4 %collective-permute-start.5 = (bf16[4,128,256]{2,1,0:T(8,128)(2,1)S(1)}, bf16[4,128,256]{2,1,0:T(8,128)(2,1)S(1)}, u32[]{:S(2)}, u32[]{:S(2)}) collective-permute-start(bf16[4,128,256]{2,1,0:T(8,128)(2,1)S(1)} %get-tuple-element.26), channel_id=1, source_target_pairs={{0,64},{64,0},{128,192},{192,128},{256,320},{320,256},{384,448},{4... | collective-permute-start | bytes 786440 | tf_op jit(solution)/shard_map/ppermute | solution.py:190
  77.2 10.1 %collective-permute-start.6 = (bf16[128,256]{1,0:T(8,128)(2,1)S(1)}, bf16[128,256]{1,0:T(8,128)(2,1)S(1)}, u32[]{:S(2)}, u32[]{:S(2)}) collective-permute-start(bf16[128,256]{1,0:T(8,128)(2,1)S(1)} %get-tuple-element.28), channel_id=1, source_target_pairs={{0,128},{64,192},{128,0},{192,64},{256,384},{320,448},{384,256},{4... | collective-permute-start | bytes 196616 | tf_op jit(solution)/shard_map/ppermute | solution.py:190
  79.5 8.5 %collective-permute-start.7 = (bf16[128,256]{1,0:T(8,128)(2,1)S(1)}, bf16[128,256]{1,0:T(8,128)(2,1)S(1)}, u32[]{:S(2)}, u32[]{:S(2)}) collective-permute-start(bf16[128,256]{1,0:T(8,128)(2,1)S(1)} %get-tuple-element.29), channel_id=1, source_target_pairs={{0,256},{64,320},{128,384},{192,448},{256,0},{320,64},{384,128},{4... | collective-permute-start | bytes 196616 | tf_op jit(solution)/shard_map/ppermute | solution.py:190
  84.5 8.0 %collective-permute-start.8 = (bf16[128,256]{1,0:T(8,128)(2,1)S(1)}, bf16[128,256]{1,0:T(8,128)(2,1)S(1)}, u32[]{:S(2)}, u32[]{:S(2)}) collective-permute-start(bf16[128,256]{1,0:T(8,128)(2,1)S(1)} %get-tuple-element.30), channel_id=1, source_target_pairs={{0,384},{64,448},{128,256},{192,320},{256,128},{320,192},{384,0},{... | collective-permute-start | bytes 196616 | tf_op jit(solution)/shard_map/ppermute | solution.py:190

commit v4 on v3

--- a/solution.py
+++ b/solution.py
@@ -60,13 +60,11 @@
     tiles = [slot[:, start : start + LANES] for start in range(0, SLOT, LANES)]
     tiles.append(jnp.zeros((swap_ref.shape[0] - 4 * across - SLOT // LANES * own_in, LANES), F32))
     swap_ref[4 * across :] = jnp.concatenate(tiles, axis=0).astype(BF16)
-    body_ref[:, :channels] = jnp.broadcast_to(
-        jax.nn.silu(inputs_ref[...].reshape(-1, channels).astype(F32)).T.astype(BF16)[None],
-        (CHIPS, channels, LANES),
-    )
+    body_ref[:channels] = jax.nn.silu(inputs_ref[...].reshape(-1, channels).astype(F32)).T.astype(BF16)
     halves = [cot_ref[frame].reshape(-1, channels).astype(F32) for frame in range(2)]
     for target in range(CHIPS):
-        body_ref[target, channels:] = for_chip(target, halves[0], halves[1])
+        part = for_chip(target, halves[0], halves[1])
+        body_ref[channels + part.shape[0] * target : channels + part.shape[0] * (target + 1)] = part
 
 
 def joined(own_ref, swapped_ref, blocks_ref):
@@ -98,8 +96,10 @@
 def pack(body_ref, first_ref, second_ref, *out_and_scratch):
     outs, halo = out_and_scratch[:CHIPS], out_and_scratch[CHIPS]
     chip, _ = chip_and_core()
-    rows = body_ref.shape[1]
     across = 16
+    rows = outs[0].shape[0] - 2 * across
+    channels = 256
+    held = rows - channels
     odd = lax.axis_index("rows") % 2
     for side, ref in ((1 - odd, first_ref), (odd, second_ref)):
         tiles = [ref[across * tile : across * tile + across].astype(F32) for tile in range(4)]
@@ -108,7 +108,9 @@
             part = halved(target, tiles[tile], tiles[2 + tile])
             halo[target, pl.ds(pl.multiple_of(across * side, across), across)] = part
     for step, out in enumerate(outs):
-        out[:rows] = body_ref[chip ^ step]
+        out[:channels] = body_ref[:channels]
+        start = pl.multiple_of(channels + held * (chip ^ step), held)
+        out[channels:rows] = body_ref[pl.ds(start, held)]
         out[rows:] = halo[chip ^ step]
 
 
@@ -150,18 +152,25 @@
     terms_ref[...] = terms.reshape(terms_ref.shape).astype(BF16)
 
 
-def transposed(windows_ref, kernel_ref, keep_ref, give_ref, wide, product):
+def given(windows_ref, kernel_ref, give_ref, wide):
     chip, core = chip_and_core()
     bands, own_in, _ = kernel_ref.shape
     flat = kernel_ref[...].astype(F32).reshape(bands * own_in, SLOT)
     for index in range(9):
         wide[:, LANES * index : LANES * index + LANES] = flat[:, 3 * OWN * index : 3 * OWN * index + LANES].astype(BF16)
-    product[...] = lax.dot_general(
-        windows_ref[...], wide[...], (((1,), (1,)), ((), ())), preferred_element_type=F32
-    ).reshape(product.shape)
     for step in range(CHIPS):
-        keep_ref[step] = product[CORES * (chip ^ step) + core]
-        give_ref[step] = product[CORES * (chip ^ step) + 1 - core].astype(BF16)
+        give_ref[step] = partial_of(windows_ref, wide, CORES * (chip ^ step) + 1 - core).astype(BF16)
+
+
+def kept(windows_ref, wide_ref, keep_ref):
+    chip, core = chip_and_core()
+    for step in range(CHIPS):
+        keep_ref[step] = partial_of(windows_ref, wide_ref, CORES * (chip ^ step) + core)
+
+
+def partial_of(windows_ref, wide_ref, owner):
+    rows = windows_ref[pl.ds(pl.multiple_of(LANES * owner, LANES), LANES)]
+    return lax.dot_general(rows, wide_ref[...], (((1,), (1,)), ((), ())), preferred_element_type=F32)
 
 
 def paired(keep_ref, given_ref, own_ref, *outs):
@@ -179,10 +188,16 @@
     out_ref[...] = (cot_ref[...].astype(F32) + total * slope).astype(BF16)
 
 
-def summed(terms_ref, out_ref):
-    total = jnp.sum(terms_ref[...].astype(F32), axis=0)
+def summed(terms_ref, own_ref, other_ref):
+    odd = lax.axis_index("rows") % 2
+    own_ref[...] = jnp.sum(terms_ref[:, odd].astype(F32), axis=0)
+    other_ref[...] = jnp.sum(terms_ref[:, 1 - odd].astype(F32), axis=0)
+
+
+def total(own_ref, other_ref, out_ref):
+    values = own_ref[...] + other_ref[...]
     for tap in range(TAPS):
-        out_ref[tap] = total[:, OWN * tap : OWN * tap + OWN]
+        out_ref[tap] = values[:, OWN * tap : OWN * tap + OWN]
 
 
 def stepped(block, step):
@@ -198,6 +213,10 @@
     )
 
 
+def alike(bands):
+    return [[2 * i + odd for i in range(bands // 2)] for odd in range(2)]
+
+
 def exchanged(blocks, groups):
     return lax.all_to_all(
         blocks, "rows", split_axis=0, concat_axis=0, tiled=True, axis_index_groups=groups
@@ -215,7 +234,7 @@
         prepare,
         [
             array((4 * across + LANES // 4, LANES)), array((4 * across, LANES)),
-            array((CHIPS, channels + held, LANES)),
+            array((channels + CHIPS * held, LANES)),
         ],
         kernel, inputs, cotangent, limit=60,
     )
@@ -251,21 +270,25 @@
         scratch=[pltpu.VMEM((channels, GROUPS * points), BF16), pltpu.VMEM((frames * GROUPS + 2, span, LANES), BF16)],
         flops=2 * GROUPS * points * WIDE * channels,
     )
-    terms = exchanged(terms, None)
-
-    keep, give = called(
-        transposed, [array((CHIPS, points, channels), F32), array((CHIPS, points, channels))],
-        windows, kernel_in,
-        scratch=[pltpu.VMEM((channels, WIDE), BF16), pltpu.VMEM((GROUPS, points, channels), F32)],
-        flops=2 * GROUPS * points * WIDE * channels,
-    )
-    given = stepped(give, 1)
+    terms = exchanged(terms.reshape(bands // 2, 2, own_in, SLOT), alike(bands))
+
+    give, wide = called(
+        given, [array((CHIPS, points, channels)), array((channels, WIDE))], windows, kernel_in,
+        flops=GROUPS * points * WIDE * channels,
+    )
+    give = stepped(give, 1)
+    keep, = called(
+        kept, [array((CHIPS, points, channels), F32)], windows, wide,
+        flops=GROUPS * points * WIDE * channels,
+    )
     own, *sums = called(
-        paired, [array((points, channels), F32)] + [array((points, channels))] * 3, keep, given
+        paired, [array((points, channels), F32)] + [array((points, channels))] * 3, keep, give
     )
     sums = [stepped(part, CORES * step) for step, part in enumerate(sums, 1)]
+    mine, other = called(summed, [array((own_in, SLOT), F32)] * 2, terms)
+    other = lax.ppermute(other, "rows", [(i, i ^ 1) for i in range(bands)])
     grad_inputs, = called(finish, [array(inputs.shape)], own, *sums, inputs, cotangent)
-    grad_kernel, = called(summed, [array(kernel.shape, F32)], terms)
+    grad_kernel, = called(total, [array(kernel.shape, F32)], mine, other)
     return (grad_inputs, grad_kernel)
 
 

time: 94.8 us -> 94.7 us (level)
  the two profiles are of different devices: /device:TPU:62 before, /device:TPU:64 now
where the time goes in v4:
time: 94.7 us; the launch traced here: 94 us
  starting transfers between devices  66.8 us (71%)
  waiting for transfers between devices  13.2 us (14%)
  Pallas kernels  7.45 us (8%)
  local copies, waits for them, and re-layouts  3.34 us (4%)
  blocking collectives  2.32 us (2%)
    all_to_all x3, starting transfers between devices, exchanged(): lax.all_to_all(blocks, 'rows', split_axis=0, concat_axis=0, tiled=True, a...  23.4 us
    ppermute x7, starting transfers between devices, stepped(): return lax.ppermute(block, 'tm', [(i, i ^ step) for i in range(count)])  22.1 us
    ppermute x1, starting transfers between devices, local(): first = lax.ppermute(swap, 'rows', [(i, i ^ 1) for i in range(bands)])  7.72 us
    pallas_call x10, Pallas kernels, called(): pl.pallas_call(body, out_shape=outs, in_specs=[whole] * len(args), out_sp...  7.45 us
    ppermute x1, starting transfers between devices, local(): second = lax.ppermute(second, 'rows', pairs + [(b, a) for a, b in pairs])  7.23 us
    ppermute x1, starting transfers between devices, local(): other = lax.ppermute(other, 'rows', [(i, i ^ 1) for i in range(bands)])  6.27 us
    all_to_all x3, waiting for transfers between devices, exchanged(): lax.all_to_all(blocks, 'rows', split_axis=0, concat_axis=0, tiled=True, a...  3.78 us
    ppermute x1, waiting for transfers between devices, local(): second = lax.ppermute(second, 'rows', pairs + [(b, a) for a, b in pairs])  3.4 us
  transfers between devices with their start and end apart: 13, of which 7 were waited for; matrix products, arithmetic and copies ran while one was open for 1% of the time, Pallas kernels for 5%

profile of v4, /device:TPU:64, one launch (start us, length us, event | category | flops | bytes accessed | tf_op | source)
XLA Modules:
  0.0 94.0 jit_solution(6759575114284987079)
XLA Ops:
  0.6 1.7 %shard_map.50 = (bf16[96,128]{1,0:T(8,128)(2,1)}, bf16[64,128]{1,0:T(8,128)(2,1)}, bf16[512,128]{1,0:T(8,128)(2,1)}) custom-call(bf16[27,4,32]{2,1,0:T(4,128)(2,1)} %kernel_ref.1, bf16[2,4,16,256]{3,2,1,0:T(8,128)(2,1)} %inputs_ref.3, bf16[2,4,16,256]{3,2,1,0:T(8,128)(2,1)} %cot_ref.3), custom_call_target="tpu_custom_call" | custom-call | bytes 310016 | tf_op jit(solution)/shard_map/pallas_call | solution.py:31
  2.3 7.7 %collective-permute-start = (bf16[96,128]{1,0:T(8,128)(2,1)}, bf16[96,128]{1,0:T(8,128)(2,1)S(1)}, u32[]{:S(2)}, u32[]{:S(2)}) collective-permute-start(bf16[96,128]{1,0:T(8,128)(2,1)} %get-tuple-element.20.own_ref), channel_id=1, source_target_pairs={{0,1},{1,0},{2,3},{3,2},{4,5},{5,4},{6,7},{7,6},{8,9},{9,8},{10,11... | collective-permute-start | bytes 73736 | tf_op jit(solution)/shard_map/ppermute | solution.py:241
  10.0 2.1 %collective-permute-done.first_ref.swapped_ref = bf16[96,128]{1,0:T(8,128)(2,1)S(1)} collective-permute-done((bf16[96,128]{1,0:T(8,128)(2,1)}, bf16[96,128]{1,0:T(8,128)(2,1)S(1)}, u32[]{:S(2)}, u32[]{:S(2)}) %collective-permute-start) | collective-permute-done | bytes 24608 | tf_op jit(solution)/shard_map/ppermute | solution.py:241
  12.1 0.7 copy-done.4
  12.9 0.7 shard_map.53
  13.5 10.0 %all-to-all-start = ((bf16[8,2,4,896]{3,2,1,0:T(4,128)(2,1)}), bf16[8,2,4,896]{3,2,1,0:T(4,128)(2,1)S(1)}, u32[]{:S(2)}, u32[]{:S(2)}) async-start(bf16[8,2,4,896]{3,2,1,0:T(4,128)(2,1)} %shard_map.53), calls=%async_computation | async-start | bytes 229376 | tf_op jit(solution)/shard_map/all_to_all | solution.py:221
  23.5 7.2 %collective-permute-start.1 = (bf16[64,128]{1,0:T(8,128)(2,1)}, bf16[64,128]{1,0:T(8,128)(2,1)S(1)}, u32[]{:S(2)}, u32[]{:S(2)}) collective-permute-start(bf16[64,128]{1,0:T(8,128)(2,1)} %get-tuple-element.21), channel_id=1, source_target_pairs={{1,2},{3,4},{5,6},{7,8},{9,10},{11,12},{13,14},{15,16},{17,18},{19... | collective-permute-start | bytes 49160 | tf_op jit(solution)/shard_map/ppermute | solution.py:243
  30.7 3.4 %collective-permute-done.1.second_ref = bf16[64,128]{1,0:T(8,128)(2,1)S(1)} collective-permute-done((bf16[64,128]{1,0:T(8,128)(2,1)}, bf16[64,128]{1,0:T(8,128)(2,1)S(1)}, u32[]{:S(2)}, u32[]{:S(2)}) %collective-permute-start.1) | collective-permute-done | bytes 16416 | tf_op jit(solution)/shard_map/ppermute | solution.py:243
  34.1 0.9 copy-done.3
  35.1 3.7 %collective-permute-start.2 = (bf16[352,128]{1,0:T(8,128)(2,1)S(1)}, bf16[352,128]{1,0:T(8,128)(2,1)S(1)}, u32[]{:S(2)}, u32[]{:S(2)}) collective-permute-start(bf16[352,128]{1,0:T(8,128)(2,1)S(1)} %get-tuple-element.23), channel_id=1, source_target_pairs={{0,128},{64,192},{128,0},{192,64},{256,384},{320,448},{384,256},{4... | collective-permute-start | bytes 270344 | tf_op jit(solution)/shard_map/ppermute | solution.py:205
  38.9 4.3 %collective-permute-start.3 = (bf16[352,128]{1,0:T(8,128)(2,1)S(1)}, bf16[352,128]{1,0:T(8,128)(2,1)S(1)}, u32[]{:S(2)}, u32[]{:S(2)}) collective-permute-start(bf16[352,128]{1,0:T(8,128)(2,1)S(1)} %get-tuple-element.24), channel_id=1, source_target_pairs={{0,256},{64,320},{128,384},{192,448},{256,0},{320,64},{384,128},{4... | collective-permute-start | bytes 270344 | tf_op jit(solution)/shard_map/ppermute | solution.py:205
  43.1 2.1 %collective-permute-start.4 = (bf16[352,128]{1,0:T(8,128)(2,1)S(1)}, bf16[352,128]{1,0:T(8,128)(2,1)S(1)}, u32[]{:S(2)}, u32[]{:S(2)}) collective-permute-start(bf16[352,128]{1,0:T(8,128)(2,1)S(1)} %get-tuple-element.25), channel_id=1, source_target_pairs={{0,384},{64,448},{128,256},{192,320},{256,128},{320,192},{384,0},{... | collective-permute-start | bytes 270344 | tf_op jit(solution)/shard_map/ppermute | solution.py:205
  45.3 0.9 broadcast_in_dim.8
  46.2 4.3 %all-to-all-start.1 = ((bf16[4,16,4,896]{3,2,1,0:T(4,128)(2,1)}), bf16[4,16,4,896]{3,2,1,0:T(4,128)(2,1)S(1)}, u32[]{:S(2)}, u32[]{:S(2)}) async-start(bf16[4,16,4,896]{3,2,1,0:T(4,128)(2,1)} %broadcast_in_dim.8), calls=%async_computation.1 | async-start | bytes 917504 | tf_op jit(solution)/shard_map/all_to_all | solution.py:221
  50.5 0.9 collective-permute-done.4
  51.4 2.3 %all-gather = bf16[8,352,128]{2,1,0:T(8,128)(2,1)S(1)} all-gather(bf16[4,352,128]{2,1,0:T(8,128)(2,1)S(1)} %pad_maximum_fusion), channel_id=2, replica_groups={{0,64},{128,192},{256,320},{384,448},{1,65},{129,193},{257,321},{385,44..., dimensions={0}, use_global_device_ids=true | all-gather | bytes 1081344 | tf_op jit(solution)/shard_map/all_gather | solution.py:259
  53.7 1.5 %shard_map.52 = (bf16[64,4,896]{2,1,0:T(4,128)(2,1)S(1)}, bf16[1024,1152]{1,0:T(8,128)(2,1)S(1)}) custom-call(bf16[2,4,352,128]{3,2,1,0:T(8,128)(2,1)S(1)} %bitcast.9), custom_call_target="tpu_custom_call" | custom-call | flops 603979776 | bytes 3538944 | tf_op jit(solution)/shard_map/pallas_call | solution.py:31
  55.3 0.8 copy-done
  56.0 2.2 %all-to-all-done.1 = bf16[4,16,4,896]{3,2,1,0:T(4,128)(2,1)S(1)} async-done(((bf16[4,16,4,896]{3,2,1,0:T(4,128)(2,1)}), bf16[4,16,4,896]{3,2,1,0:T(4,128)(2,1)S(1)}, u32[]{:S(2)}, u32[]{:S(2)}) %all-to-all-start.1) | async-done | bytes 458784 | tf_op jit(solution)/shard_map/all_to_all | solution.py:221
  58.2 9.2 %all-to-all-start.2 = ((bf16[32,2,4,896]{3,2,1,0:T(4,128)(2,1)}), bf16[32,2,4,896]{3,2,1,0:T(4,128)(2,1)S(1)}, u32[]{:S(2)}, u32[]{:S(2)}) async-start(bf16[32,2,4,896]{3,2,1,0:T(4,128)(2,1)} %bitcast.10), calls=%async_computation.2 | async-start | bytes 917504 | tf_op jit(solution)/shard_map/all_to_all | solution.py:221
  67.4 1.0 %shard_map.54 = (bf16[4,128,256]{2,1,0:T(8,128)(2,1)S(1)}, bf16[256,1152]{1,0:T(8,128)(2,1)S(1)}) custom-call(bf16[1024,1152]{1,0:T(8,128)(2,1)S(1)} %get-tuple-element.26.windows_ref, bf16[64,4,896]{2,1,0:T(4,128)(2,1)S(1)} %bitcast.8), custom_call_target="tpu_custom_call" | custom-call | flops 301989888 | bytes 3670016 | tf_op jit(solution)/shard_map/pallas_call | solution.py:31
  68.4 1.9 %collective-permute-start.5 = (bf16[4,128,256]{2,1,0:T(8,128)(2,1)S(1)}, bf16[4,128,256]{2,1,0:T(8,128)(2,1)S(1)}, u32[]{:S(2)}, u32[]{:S(2)}) collective-permute-start(bf16[4,128,256]{2,1,0:T(8,128)(2,1)S(1)} %get-tuple-element.28), channel_id=1, source_target_pairs={{0,64},{64,0},{128,192},{192,128},{256,320},{320,256},{384,448},{4... | collective-permute-start | bytes 786440 | tf_op jit(solution)/shard_map/ppermute | solution.py:205
  70.3 0.9 shard_map.55.keep_ref
  71.2 0.6 collective-permute-done.5.given_ref
  71.9 2.6 %collective-permute-start.6 = (bf16[128,256]{1,0:T(8,128)(2,1)S(1)}, bf16[128,256]{1,0:T(8,128)(2,1)S(1)}, u32[]{:S(2)}, u32[]{:S(2)}) collective-permute-start(bf16[128,256]{1,0:T(8,128)(2,1)S(1)} %get-tuple-element.30), channel_id=1, source_target_pairs={{0,128},{64,192},{128,0},{192,64},{256,384},{320,448},{384,256},{4... | collective-permute-start | bytes 196616 | tf_op jit(solution)/shard_map/ppermute | solution.py:205
  74.5 5.3 %collective-permute-start.7 = (bf16[128,256]{1,0:T(8,128)(2,1)S(1)}, bf16[128,256]{1,0:T(8,128)(2,1)S(1)}, u32[]{:S(2)}, u32[]{:S(2)}) collective-permute-start(bf16[128,256]{1,0:T(8,128)(2,1)S(1)} %get-tuple-element.31), channel_id=1, source_target_pairs={{0,256},{64,320},{128,384},{192,448},{256,0},{320,64},{384,128},{4... | collective-permute-start | bytes 196616 | tf_op jit(solution)/shard_map/ppermute | solution.py:205
  79.9 2.1 %collective-permute-start.8 = (bf16[128,256]{1,0:T(8,128)(2,1)S(1)}, bf16[128,256]{1,0:T(8,128)(2,1)S(1)}, u32[]{:S(2)}, u32[]{:S(2)}) collective-permute-start(bf16[128,256]{1,0:T(8,128)(2,1)S(1)} %get-tuple-element.32), channel_id=1, source_target_pairs={{0,384},{64,448},{128,256},{192,320},{256,128},{320,192},{384,0},{... | collective-permute-start | bytes 196616 | tf_op jit(solution)/shard_map/ppermute | solution.py:205
  82.0 1.6 %all-to-all-done.2.terms_ref = bf16[32,2,4,896]{3,2,1,0:T(4,128)(2,1)S(1)} async-done(((bf16[32,2,4,896]{3,2,1,0:T(4,128)(2,1)}), bf16[32,2,4,896]{3,2,1,0:T(4,128)(2,1)S(1)}, u32[]{:S(2)}, u32[]{:S(2)}) %all-to-all-start.2) | async-done | bytes 458784 | tf_op jit(solution)/shard_map/all_to_all | solution.py:221
  83.8 6.3 %collective-permute-start.9 = (f32[4,896]{1,0:T(4,128)S(1)}, f32[4,896]{1,0:T(4,128)S(1)}, u32[]{:S(2)}, u32[]{:S(2)}) collective-permute-start(f32[4,896]{1,0:T(4,128)S(1)} %get-tuple-element.35), channel_id=1, source_target_pairs={{0,1},{1,0},{2,3},{3,2},{4,5},{5,4},{6,7},{7,6},{8,9},{9,8},{10,11... | collective-permute-start | bytes 43016 | tf_op jit(solution)/shard_map/ppermute | solution.py:289
  90.1 0.7 shard_map.57
  90.8 2.5 %collective-permute-done.9.other_ref = f32[4,896]{1,0:T(4,128)S(1)} collective-permute-done((f32[4,896]{1,0:T(4,128)S(1)}, f32[4,896]{1,0:T(4,128)S(1)}, u32[]{:S(2)}, u32[]{:S(2)}) %collective-permute-start.9) | collective-permute-done | bytes 14368 | tf_op jit(solution)/shard_map/ppermute | solution.py:289
  93.3 0.7 shard_map.59
  (17 shorter events, 0.4 us)
Async XLA Ops:
  2.3 9.8 %collective-permute-start = (bf16[96,128]{1,0:T(8,128)(2,1)}, bf16[96,128]{1,0:T(8,128)(2,1)S(1)}, u32[]{:S(2)}, u32[]{:S(2)}) collective-permute-start(bf16[96,128]{1,0:T(8,128)(2,1)} %get-tuple-element.20.own_ref), channel_id=1, source_target_pairs={{0,1},{1,0},{2,3},{3,2},{4,5},{5,4},{6,7},{7,6},{8,9},{9,8},{10,11... | collective-permute-start | bytes 73736 | tf_op jit(solution)/shard_map/ppermute | solution.py:241
  12.1 0.7 copy-start.4
  13.5 31.7 %all-to-all-start = ((bf16[8,2,4,896]{3,2,1,0:T(4,128)(2,1)}), bf16[8,2,4,896]{3,2,1,0:T(4,128)(2,1)S(1)}, u32[]{:S(2)}, u32[]{:S(2)}) async-start(bf16[8,2,4,896]{3,2,1,0:T(4,128)(2,1)} %shard_map.53), calls=%async_computation | async-start | bytes 229376 | tf_op jit(solution)/shard_map/all_to_all | solution.py:221
  23.5 10.6 %collective-permute-start.1 = (bf16[64,128]{1,0:T(8,128)(2,1)}, bf16[64,128]{1,0:T(8,128)(2,1)S(1)}, u32[]{:S(2)}, u32[]{:S(2)}) collective-permute-start(bf16[64,128]{1,0:T(8,128)(2,1)} %get-tuple-element.21), channel_id=1, source_target_pairs={{1,2},{3,4},{5,6},{7,8},{9,10},{11,12},{13,14},{15,16},{17,18},{19... | collective-permute-start | bytes 49160 | tf_op jit(solution)/shard_map/ppermute | solution.py:243
  34.1 0.9 copy-start.3
  35.1 15.3 %collective-permute-start.2 = (bf16[352,128]{1,0:T(8,128)(2,1)S(1)}, bf16[352,128]{1,0:T(8,128)(2,1)S(1)}, u32[]{:S(2)}, u32[]{:S(2)}) collective-permute-start(bf16[352,128]{1,0:T(8,128)(2,1)S(1)} %get-tuple-element.23), channel_id=1, source_target_pairs={{0,128},{64,192},{128,0},{192,64},{256,384},{320,448},{384,256},{4... | collective-permute-start | bytes 270344 | tf_op jit(solution)/shard_map/ppermute | solution.py:205
  38.9 11.6 %collective-permute-start.3 = (bf16[352,128]{1,0:T(8,128)(2,1)S(1)}, bf16[352,128]{1,0:T(8,128)(2,1)S(1)}, u32[]{:S(2)}, u32[]{:S(2)}) collective-permute-start(bf16[352,128]{1,0:T(8,128)(2,1)S(1)} %get-tuple-element.24), channel_id=1, source_target_pairs={{0,256},{64,320},{128,384},{192,448},{256,0},{320,64},{384,128},{4... | collective-permute-start | bytes 270344 | tf_op jit(solution)/shard_map/ppermute | solution.py:205
  43.1 8.2 %collective-permute-start.4 = (bf16[352,128]{1,0:T(8,128)(2,1)S(1)}, bf16[352,128]{1,0:T(8,128)(2,1)S(1)}, u32[]{:S(2)}, u32[]{:S(2)}) collective-permute-start(bf16[352,128]{1,0:T(8,128)(2,1)S(1)} %get-tuple-element.25), channel_id=1, source_target_pairs={{0,384},{64,448},{128,256},{192,320},{256,128},{320,192},{384,0},{... | collective-permute-start | bytes 270344 | tf_op jit(solution)/shard_map/ppermute | solution.py:205
  46.2 12.0 %all-to-all-start.1 = ((bf16[4,16,4,896]{3,2,1,0:T(4,128)(2,1)}), bf16[4,16,4,896]{3,2,1,0:T(4,128)(2,1)S(1)}, u32[]{:S(2)}, u32[]{:S(2)}) async-start(bf16[4,16,4,896]{3,2,1,0:T(4,128)(2,1)} %broadcast_in_dim.8), calls=%async_computation.1 | async-start | bytes 917504 | tf_op jit(solution)/shard_map/all_to_all | solution.py:221
  55.3 0.8 copy-start
  58.2 25.4 %all-to-all-start.2 = ((bf16[32,2,4,896]{3,2,1,0:T(4,128)(2,1)}), bf16[32,2,4,896]{3,2,1,0:T(4,128)(2,1)S(1)}, u32[]{:S(2)}, u32[]{:S(2)}) async-start(bf16[32,2,4,896]{3,2,1,0:T(4,128)(2,1)} %bitcast.10), calls=%async_computation.2 | async-start | bytes 917504 | tf_op jit(solution)/shard_map/all_to_all | solution.py:221
  68.4 3.4 %collective-permute-start.5 = (bf16[4,128,256]{2,1,0:T(8,128)(2,1)S(1)}, bf16[4,128,256]{2,1,0:T(8,128)(2,1)S(1)}, u32[]{:S(2)}, u32[]{:S(2)}) collective-permute-start(bf16[4,128,256]{2,1,0:T(8,128)(2,1)S(1)} %get-tuple-element.28), channel_id=1, source_target_pairs={{0,64},{64,0},{128,192},{192,128},{256,320},{320,256},{384,448},{4... | collective-permute-start | bytes 786440 | tf_op jit(solution)/shard_map/ppermute | solution.py:205
  70.3 19.8 %copy-start.1 = (bf16[2,4,16,256]{3,2,1,0:T(8,128)(2,1)S(1)}, bf16[2,4,16,256]{3,2,1,0:T(8,128)(2,1)}, u32[]{:S(2)}) copy-start(bf16[2,4,16,256]{3,2,1,0:T(8,128)(2,1)} %inputs_ref.3) | copy-start | bytes 196612
  70.3 19.8 %copy-start.2 = (bf16[2,4,16,256]{3,2,1,0:T(8,128)(2,1)S(1)}, bf16[2,4,16,256]{3,2,1,0:T(8,128)(2,1)}, u32[]{:S(2)}) copy-start(bf16[2,4,16,256]{3,2,1,0:T(8,128)(2,1)} %cot_ref.3) | copy-start | bytes 196612
  71.9 18.2 %collective-permute-start.6 = (bf16[128,256]{1,0:T(8,128)(2,1)S(1)}, bf16[128,256]{1,0:T(8,128)(2,1)S(1)}, u32[]{:S(2)}, u32[]{:S(2)}) collective-permute-start(bf16[128,256]{1,0:T(8,128)(2,1)S(1)} %get-tuple-element.30), channel_id=1, source_target_pairs={{0,128},{64,192},{128,0},{192,64},{256,384},{320,448},{384,256},{4... | collective-permute-start | bytes 196616 | tf_op jit(solution)/shard_map/ppermute | solution.py:205
  74.5 15.6 %collective-permute-start.7 = (bf16[128,256]{1,0:T(8,128)(2,1)S(1)}, bf16[128,256]{1,0:T(8,128)(2,1)S(1)}, u32[]{:S(2)}, u32[]{:S(2)}) collective-permute-start(bf16[128,256]{1,0:T(8,128)(2,1)S(1)} %get-tuple-element.31), channel_id=1, source_target_pairs={{0,256},{64,320},{128,384},{192,448},{256,0},{320,64},{384,128},{4... | collective-permute-start | bytes 196616 | tf_op jit(solution)/shard_map/ppermute | solution.py:205
  79.9 10.3 %collective-permute-start.8 = (bf16[128,256]{1,0:T(8,128)(2,1)S(1)}, bf16[128,256]{1,0:T(8,128)(2,1)S(1)}, u32[]{:S(2)}, u32[]{:S(2)}) collective-permute-start(bf16[128,256]{1,0:T(8,128)(2,1)S(1)} %get-tuple-element.32), channel_id=1, source_target_pairs={{0,384},{64,448},{128,256},{192,320},{256,128},{320,192},{384,0},{... | collective-permute-start | bytes 196616 | tf_op jit(solution)/shard_map/ppermute | solution.py:205
  83.8 9.5 %collective-permute-start.9 = (f32[4,896]{1,0:T(4,128)S(1)}, f32[4,896]{1,0:T(4,128)S(1)}, u32[]{:S(2)}, u32[]{:S(2)}) collective-permute-start(f32[4,896]{1,0:T(4,128)S(1)} %get-tuple-element.35), channel_id=1, source_target_pairs={{0,1},{1,0},{2,3},{3,2},{4,5},{5,4},{6,7},{7,6},{8,9},{9,8},{10,11... | collective-permute-start | bytes 43016 | tf_op jit(solution)/shard_map/ppermute | solution.py:289

commit v5 on v4

--- a/solution.py
+++ b/solution.py
@@ -152,31 +152,25 @@
     terms_ref[...] = terms.reshape(terms_ref.shape).astype(BF16)
 
 
-def given(windows_ref, kernel_ref, give_ref, wide):
+def transposed(windows_ref, kernel_ref, keep_ref, give_ref, wide, product):
     chip, core = chip_and_core()
     bands, own_in, _ = kernel_ref.shape
     flat = kernel_ref[...].astype(F32).reshape(bands * own_in, SLOT)
     for index in range(9):
         wide[:, LANES * index : LANES * index + LANES] = flat[:, 3 * OWN * index : 3 * OWN * index + LANES].astype(BF16)
+    product[...] = lax.dot_general(
+        windows_ref[...], wide[...], (((1,), (1,)), ((), ())), preferred_element_type=F32
+    ).reshape(product.shape)
     for step in range(CHIPS):
-        give_ref[step] = partial_of(windows_ref, wide, CORES * (chip ^ step) + 1 - core).astype(BF16)
-
-
-def kept(windows_ref, wide_ref, keep_ref):
-    chip, core = chip_and_core()
-    for step in range(CHIPS):
-        keep_ref[step] = partial_of(windows_ref, wide_ref, CORES * (chip ^ step) + core)
-
-
-def partial_of(windows_ref, wide_ref, owner):
-    rows = windows_ref[pl.ds(pl.multiple_of(LANES * owner, LANES), LANES)]
-    return lax.dot_general(rows, wide_ref[...], (((1,), (1,)), ((), ())), preferred_element_type=F32)
+        keep_ref[step] = product[CORES * (chip ^ step) + core]
+        give_ref[step] = product[CORES * (chip ^ step) + 1 - core].astype(BF16)
 
 
 def paired(keep_ref, given_ref, own_ref, *outs):
-    own_ref[...] = keep_ref[0] + given_ref[0].astype(F32)
+    _, core = chip_and_core()
+    own_ref[...] = keep_ref[0] + given_ref[1 - core, 0].astype(F32)
     for step, out in enumerate(outs, 1):
-        out[...] = (keep_ref[step] + given_ref[step].astype(F32)).astype(BF16)
+        out[...] = (keep_ref[step] + given_ref[1 - core, step].astype(F32)).astype(BF16)
 
 
 def finish(own_ref, first_ref, second_ref, third_ref, inputs_ref, cot_ref, out_ref):
@@ -272,17 +266,15 @@
     )
     terms = exchanged(terms.reshape(bands // 2, 2, own_in, SLOT), alike(bands))
 
-    give, wide = called(
-        given, [array((CHIPS, points, channels)), array((channels, WIDE))], windows, kernel_in,
-        flops=GROUPS * points * WIDE * channels,
-    )
-    give = stepped(give, 1)
-    keep, = called(
-        kept, [array((CHIPS, points, channels), F32)], windows, wide,
-        flops=GROUPS * points * WIDE * channels,
-    )
+    keep, give = called(
+        transposed, [array((CHIPS, points, channels), F32), array((CHIPS, points, channels))],
+        windows, kernel_in,
+        scratch=[pltpu.VMEM((channels, WIDE), BF16), pltpu.VMEM((GROUPS, points, channels), F32)],
+        flops=2 * GROUPS * points * WIDE * channels,
+    )
+    given = lax.all_gather(give, "tm", axis=0, axis_index_groups=PAIRS)
     own, *sums = called(
-        paired, [array((points, channels), F32)] + [array((points, channels))] * 3, keep, give
+        paired, [array((points, channels), F32)] + [array((points, channels))] * 3, keep, given
     )
     sums = [stepped(part, CORES * step) for step, part in enumerate(sums, 1)]
     mine, other = called(summed, [array((own_in, SLOT), F32)] * 2, terms)

time: 94.7 us -> 94.7 us (level)
  blocking collectives: 2.32 us -> 4.5 us
  starting transfers between devices: 66.8 us -> 64.9 us
    all_gather x0 -> x1, blocking collectives: none -> 2.18 us  [local(): given = lax.all_gather(give, 'tm', axis=0, axis_index_groups=PAIRS)]
    ppermute x7 -> x6, starting transfers between devices: 22.1 us -> 20.2 us  [stepped(): return lax.ppermute(block, 'tm', [(i, i ^ step) for i in range(count)])]
    all_to_all x3, waiting for transfers between devices: 3.78 us -> 4.9 us  [exchanged(): lax.all_to_all(blocks, 'rows', split_axis=0, concat_axis=0, tiled=True, a...]
    pallas_call x10 -> x9, Pallas kernels: 7.45 us -> 6.7 us  [called(): pl.pallas_call(body, out_shape=outs, in_specs=[whole] * len(args), out_sp...]
  transfers between devices with their start and end apart: 13 -> 12, of which waited for: 7 -> 6; matrix products, arithmetic and copies ran while one was open for 1% -> 1% of each run, Pallas kernels for 5% -> 4%
where the time goes in v5:
time: 94.7 us; the launch traced here: 94 us
  starting transfers between devices  64.9 us (69%)
  waiting for transfers between devices  13.8 us (15%)
  Pallas kernels  6.7 us (7%)
  blocking collectives  4.5 us (5%)
  local copies, waits for them, and re-layouts  3.33 us (4%)
    all_to_all x3, starting transfers between devices, exchanged(): lax.all_to_all(blocks, 'rows', split_axis=0, concat_axis=0, tiled=True, a...  23.4 us
    ppermute x6, starting transfers between devices, stepped(): return lax.ppermute(block, 'tm', [(i, i ^ step) for i in range(count)])  20.2 us
    ppermute x1, starting transfers between devices, local(): first = lax.ppermute(swap, 'rows', [(i, i ^ 1) for i in range(bands)])  7.72 us
    ppermute x1, starting transfers between devices, local(): second = lax.ppermute(second, 'rows', pairs + [(b, a) for a, b in pairs])  7.23 us
    pallas_call x9, Pallas kernels, called(): pl.pallas_call(body, out_shape=outs, in_specs=[whole] * len(args), out_sp...  6.7 us
    ppermute x1, starting transfers between devices, local(): other = lax.ppermute(other, 'rows', [(i, i ^ 1) for i in range(bands)])  6.25 us
    all_to_all x3, waiting for transfers between devices, exchanged(): lax.all_to_all(blocks, 'rows', split_axis=0, concat_axis=0, tiled=True, a...  4.9 us
    ppermute x1, waiting for transfers between devices, local(): second = lax.ppermute(second, 'rows', pairs + [(b, a) for a, b in pairs])  3.4 us
  transfers between devices with their start and end apart: 12, of which 6 were waited for; matrix products, arithmetic and copies ran while one was open for 1% of the time, Pallas kernels for 4%

profile of v5, /device:TPU:64, one launch (start us, length us, event | category | flops | bytes accessed | tf_op | source)
XLA Modules:
  0.0 94.0 jit_solution(12471465051374696484)
XLA Ops:
  0.6 1.7 %shard_map.50 = (bf16[96,128]{1,0:T(8,128)(2,1)}, bf16[64,128]{1,0:T(8,128)(2,1)}, bf16[512,128]{1,0:T(8,128)(2,1)}) custom-call(bf16[27,4,32]{2,1,0:T(4,128)(2,1)} %kernel_ref.1, bf16[2,4,16,256]{3,2,1,0:T(8,128)(2,1)} %inputs_ref.3, bf16[2,4,16,256]{3,2,1,0:T(8,128)(2,1)} %cot_ref.3), custom_call_target="tpu_custom_call" | custom-call | bytes 310016 | tf_op jit(solution)/shard_map/pallas_call | solution.py:31
  2.3 7.7 %collective-permute-start = (bf16[96,128]{1,0:T(8,128)(2,1)}, bf16[96,128]{1,0:T(8,128)(2,1)S(1)}, u32[]{:S(2)}, u32[]{:S(2)}) collective-permute-start(bf16[96,128]{1,0:T(8,128)(2,1)} %get-tuple-element.20.own_ref), channel_id=1, source_target_pairs={{0,1},{1,0},{2,3},{3,2},{4,5},{5,4},{6,7},{7,6},{8,9},{9,8},{10,11... | collective-permute-start | bytes 73736 | tf_op jit(solution)/shard_map/ppermute | solution.py:235
  10.0 2.1 %collective-permute-done.first_ref.swapped_ref = bf16[96,128]{1,0:T(8,128)(2,1)S(1)} collective-permute-done((bf16[96,128]{1,0:T(8,128)(2,1)}, bf16[96,128]{1,0:T(8,128)(2,1)S(1)}, u32[]{:S(2)}, u32[]{:S(2)}) %collective-permute-start) | collective-permute-done | bytes 24608 | tf_op jit(solution)/shard_map/ppermute | solution.py:235
  12.1 0.7 copy-done.4
  12.9 0.7 shard_map.53
  13.5 10.0 %all-to-all-start = ((bf16[8,2,4,896]{3,2,1,0:T(4,128)(2,1)}), bf16[8,2,4,896]{3,2,1,0:T(4,128)(2,1)S(1)}, u32[]{:S(2)}, u32[]{:S(2)}) async-start(bf16[8,2,4,896]{3,2,1,0:T(4,128)(2,1)} %shard_map.53), calls=%async_computation | async-start | bytes 229376 | tf_op jit(solution)/shard_map/all_to_all | solution.py:215
  23.5 7.2 %collective-permute-start.1 = (bf16[64,128]{1,0:T(8,128)(2,1)}, bf16[64,128]{1,0:T(8,128)(2,1)S(1)}, u32[]{:S(2)}, u32[]{:S(2)}) collective-permute-start(bf16[64,128]{1,0:T(8,128)(2,1)} %get-tuple-element.21), channel_id=1, source_target_pairs={{1,2},{3,4},{5,6},{7,8},{9,10},{11,12},{13,14},{15,16},{17,18},{19... | collective-permute-start | bytes 49160 | tf_op jit(solution)/shard_map/ppermute | solution.py:237
  30.7 3.4 %collective-permute-done.1.second_ref = bf16[64,128]{1,0:T(8,128)(2,1)S(1)} collective-permute-done((bf16[64,128]{1,0:T(8,128)(2,1)}, bf16[64,128]{1,0:T(8,128)(2,1)S(1)}, u32[]{:S(2)}, u32[]{:S(2)}) %collective-permute-start.1) | collective-permute-done | bytes 16416 | tf_op jit(solution)/shard_map/ppermute | solution.py:237
  34.1 0.9 copy-done.3
  35.0 0.1 shard_map.51
  35.1 3.7 %collective-permute-start.2 = (bf16[352,128]{1,0:T(8,128)(2,1)S(1)}, bf16[352,128]{1,0:T(8,128)(2,1)S(1)}, u32[]{:S(2)}, u32[]{:S(2)}) collective-permute-start(bf16[352,128]{1,0:T(8,128)(2,1)S(1)} %get-tuple-element.23), channel_id=1, source_target_pairs={{0,128},{64,192},{128,0},{192,64},{256,384},{320,448},{384,256},{4... | collective-permute-start | bytes 270344 | tf_op jit(solution)/shard_map/ppermute | solution.py:199
  38.9 4.3 %collective-permute-start.3 = (bf16[352,128]{1,0:T(8,128)(2,1)S(1)}, bf16[352,128]{1,0:T(8,128)(2,1)S(1)}, u32[]{:S(2)}, u32[]{:S(2)}) collective-permute-start(bf16[352,128]{1,0:T(8,128)(2,1)S(1)} %get-tuple-element.24), channel_id=1, source_target_pairs={{0,256},{64,320},{128,384},{192,448},{256,0},{320,64},{384,128},{4... | collective-permute-start | bytes 270344 | tf_op jit(solution)/shard_map/ppermute | solution.py:199
  43.1 2.1 %collective-permute-start.4 = (bf16[352,128]{1,0:T(8,128)(2,1)S(1)}, bf16[352,128]{1,0:T(8,128)(2,1)S(1)}, u32[]{:S(2)}, u32[]{:S(2)}) collective-permute-start(bf16[352,128]{1,0:T(8,128)(2,1)S(1)} %get-tuple-element.25), channel_id=1, source_target_pairs={{0,384},{64,448},{128,256},{192,320},{256,128},{320,192},{384,0},{... | collective-permute-start | bytes 270344 | tf_op jit(solution)/shard_map/ppermute | solution.py:199
  45.3 0.9 broadcast_in_dim.8
  46.2 4.3 %all-to-all-start.1 = ((bf16[4,16,4,896]{3,2,1,0:T(4,128)(2,1)}), bf16[4,16,4,896]{3,2,1,0:T(4,128)(2,1)S(1)}, u32[]{:S(2)}, u32[]{:S(2)}) async-start(bf16[4,16,4,896]{3,2,1,0:T(4,128)(2,1)} %broadcast_in_dim.8), calls=%async_computation.1 | async-start | bytes 917504 | tf_op jit(solution)/shard_map/all_to_all | solution.py:215
  50.5 0.9 collective-permute-done.4
  51.4 2.3 %all-gather = bf16[8,352,128]{2,1,0:T(8,128)(2,1)S(1)} all-gather(bf16[4,352,128]{2,1,0:T(8,128)(2,1)S(1)} %pad_maximum_fusion), channel_id=2, replica_groups={{0,64},{128,192},{256,320},{384,448},{1,65},{129,193},{257,321},{385,44..., dimensions={0}, use_global_device_ids=true | all-gather | bytes 1081344 | tf_op jit(solution)/shard_map/all_gather | solution.py:253
  53.7 1.5 %shard_map.52 = (bf16[64,4,896]{2,1,0:T(4,128)(2,1)S(1)}, bf16[1024,1152]{1,0:T(8,128)(2,1)S(1)}) custom-call(bf16[2,4,352,128]{3,2,1,0:T(8,128)(2,1)S(1)} %bitcast.11), custom_call_target="tpu_custom_call" | custom-call | flops 603979776 | bytes 3538944 | tf_op jit(solution)/shard_map/pallas_call | solution.py:31
  55.3 0.8 copy-done
  56.0 2.1 %all-to-all-done.1 = bf16[4,16,4,896]{3,2,1,0:T(4,128)(2,1)S(1)} async-done(((bf16[4,16,4,896]{3,2,1,0:T(4,128)(2,1)}), bf16[4,16,4,896]{3,2,1,0:T(4,128)(2,1)S(1)}, u32[]{:S(2)}, u32[]{:S(2)}) %all-to-all-start.1) | async-done | bytes 458784 | tf_op jit(solution)/shard_map/all_to_all | solution.py:215
  58.2 9.2 %all-to-all-start.2 = ((bf16[32,2,4,896]{3,2,1,0:T(4,128)(2,1)}), bf16[32,2,4,896]{3,2,1,0:T(4,128)(2,1)S(1)}, u32[]{:S(2)}, u32[]{:S(2)}) async-start(bf16[32,2,4,896]{3,2,1,0:T(4,128)(2,1)} %bitcast.12), calls=%async_computation.2 | async-start | bytes 917504 | tf_op jit(solution)/shard_map/all_to_all | solution.py:215
  67.4 1.1 %shard_map.54 = (f32[4,128,256]{2,1,0:T(8,128)S(1)}, bf16[4,128,256]{2,1,0:T(8,128)(2,1)S(1)}) custom-call(bf16[1024,1152]{1,0:T(8,128)(2,1)S(1)} %get-tuple-element.26.windows_ref, bf16[64,4,896]{2,1,0:T(4,128)(2,1)S(1)} %bitcast.10), custom_call_target="tpu_custom_call" | custom-call | flops 603979776 | bytes 3604480 | tf_op jit(solution)/shard_map/pallas_call | solution.py:31
  68.5 2.2 %all-gather.1 = bf16[8,128,256]{2,1,0:T(8,128)(2,1)S(1)} all-gather(bf16[4,128,256]{2,1,0:T(8,128)(2,1)S(1)} %get-tuple-element.28), channel_id=3, replica_groups={{0,64},{128,192},{256,320},{384,448},{1,65},{129,193},{257,321},{385,44..., dimensions={0}, use_global_device_ids=true | all-gather | bytes 786432 | tf_op jit(solution)/shard_map/all_gather | solution.py:275
  70.7 2.6 %collective-permute-start.5 = (bf16[128,256]{1,0:T(8,128)(2,1)S(1)}, bf16[128,256]{1,0:T(8,128)(2,1)S(1)}, u32[]{:S(2)}, u32[]{:S(2)}) collective-permute-start(bf16[128,256]{1,0:T(8,128)(2,1)S(1)} %get-tuple-element.30), channel_id=1, source_target_pairs={{0,128},{64,192},{128,0},{192,64},{256,384},{320,448},{384,256},{4... | collective-permute-start | bytes 196616 | tf_op jit(solution)/shard_map/ppermute | solution.py:199
  73.4 5.3 %collective-permute-start.6 = (bf16[128,256]{1,0:T(8,128)(2,1)S(1)}, bf16[128,256]{1,0:T(8,128)(2,1)S(1)}, u32[]{:S(2)}, u32[]{:S(2)}) collective-permute-start(bf16[128,256]{1,0:T(8,128)(2,1)S(1)} %get-tuple-element.31), channel_id=1, source_target_pairs={{0,256},{64,320},{128,384},{192,448},{256,0},{320,64},{384,128},{4... | collective-permute-start | bytes 196616 | tf_op jit(solution)/shard_map/ppermute | solution.py:199
  78.7 2.1 %collective-permute-start.7 = (bf16[128,256]{1,0:T(8,128)(2,1)S(1)}, bf16[128,256]{1,0:T(8,128)(2,1)S(1)}, u32[]{:S(2)}, u32[]{:S(2)}) collective-permute-start(bf16[128,256]{1,0:T(8,128)(2,1)S(1)} %get-tuple-element.32), channel_id=1, source_target_pairs={{0,384},{64,448},{128,256},{192,320},{256,128},{320,192},{384,0},{... | collective-permute-start | bytes 196616 | tf_op jit(solution)/shard_map/ppermute | solution.py:199
  80.9 2.8 %all-to-all-done.2.terms_ref = bf16[32,2,4,896]{3,2,1,0:T(4,128)(2,1)S(1)} async-done(((bf16[32,2,4,896]{3,2,1,0:T(4,128)(2,1)}), bf16[32,2,4,896]{3,2,1,0:T(4,128)(2,1)S(1)}, u32[]{:S(2)}, u32[]{:S(2)}) %all-to-all-start.2) | async-done | bytes 458784 | tf_op jit(solution)/shard_map/all_to_all | solution.py:215
  83.6 0.2 shard_map.57
  83.8 6.2 %collective-permute-start.8 = (f32[4,896]{1,0:T(4,128)S(1)}, f32[4,896]{1,0:T(4,128)S(1)}, u32[]{:S(2)}, u32[]{:S(2)}) collective-permute-start(f32[4,896]{1,0:T(4,128)S(1)} %get-tuple-element.35), channel_id=1, source_target_pairs={{0,1},{1,0},{2,3},{3,2},{4,5},{5,4},{6,7},{7,6},{8,9},{9,8},{10,11... | collective-permute-start | bytes 43016 | tf_op jit(solution)/shard_map/ppermute | solution.py:281
  90.1 0.7 shard_map.56
  90.8 2.5 %collective-permute-done.8.other_ref = f32[4,896]{1,0:T(4,128)S(1)} collective-permute-done((f32[4,896]{1,0:T(4,128)S(1)}, f32[4,896]{1,0:T(4,128)S(1)}, u32[]{:S(2)}, u32[]{:S(2)}) %collective-permute-start.8) | collective-permute-done | bytes 14368 | tf_op jit(solution)/shard_map/ppermute | solution.py:281
  93.3 0.7 shard_map.58
  (15 shorter events, 0.1 us)
Async XLA Ops:
  2.3 9.8 %collective-permute-start = (bf16[96,128]{1,0:T(8,128)(2,1)}, bf16[96,128]{1,0:T(8,128)(2,1)S(1)}, u32[]{:S(2)}, u32[]{:S(2)}) collective-permute-start(bf16[96,128]{1,0:T(8,128)(2,1)} %get-tuple-element.20.own_ref), channel_id=1, source_target_pairs={{0,1},{1,0},{2,3},{3,2},{4,5},{5,4},{6,7},{7,6},{8,9},{9,8},{10,11... | collective-permute-start | bytes 73736 | tf_op jit(solution)/shard_map/ppermute | solution.py:235
  12.1 0.7 copy-start.4
  13.5 31.7 %all-to-all-start = ((bf16[8,2,4,896]{3,2,1,0:T(4,128)(2,1)}), bf16[8,2,4,896]{3,2,1,0:T(4,128)(2,1)S(1)}, u32[]{:S(2)}, u32[]{:S(2)}) async-start(bf16[8,2,4,896]{3,2,1,0:T(4,128)(2,1)} %shard_map.53), calls=%async_computation | async-start | bytes 229376 | tf_op jit(solution)/shard_map/all_to_all | solution.py:215
  23.5 10.6 %collective-permute-start.1 = (bf16[64,128]{1,0:T(8,128)(2,1)}, bf16[64,128]{1,0:T(8,128)(2,1)S(1)}, u32[]{:S(2)}, u32[]{:S(2)}) collective-permute-start(bf16[64,128]{1,0:T(8,128)(2,1)} %get-tuple-element.21), channel_id=1, source_target_pairs={{1,2},{3,4},{5,6},{7,8},{9,10},{11,12},{13,14},{15,16},{17,18},{19... | collective-permute-start | bytes 49160 | tf_op jit(solution)/shard_map/ppermute | solution.py:237
  34.1 0.9 copy-start.3
  35.1 15.3 %collective-permute-start.2 = (bf16[352,128]{1,0:T(8,128)(2,1)S(1)}, bf16[352,128]{1,0:T(8,128)(2,1)S(1)}, u32[]{:S(2)}, u32[]{:S(2)}) collective-permute-start(bf16[352,128]{1,0:T(8,128)(2,1)S(1)} %get-tuple-element.23), channel_id=1, source_target_pairs={{0,128},{64,192},{128,0},{192,64},{256,384},{320,448},{384,256},{4... | collective-permute-start | bytes 270344 | tf_op jit(solution)/shard_map/ppermute | solution.py:199
  38.9 11.6 %collective-permute-start.3 = (bf16[352,128]{1,0:T(8,128)(2,1)S(1)}, bf16[352,128]{1,0:T(8,128)(2,1)S(1)}, u32[]{:S(2)}, u32[]{:S(2)}) collective-permute-start(bf16[352,128]{1,0:T(8,128)(2,1)S(1)} %get-tuple-element.24), channel_id=1, source_target_pairs={{0,256},{64,320},{128,384},{192,448},{256,0},{320,64},{384,128},{4... | collective-permute-start | bytes 270344 | tf_op jit(solution)/shard_map/ppermute | solution.py:199
  43.1 8.2 %collective-permute-start.4 = (bf16[352,128]{1,0:T(8,128)(2,1)S(1)}, bf16[352,128]{1,0:T(8,128)(2,1)S(1)}, u32[]{:S(2)}, u32[]{:S(2)}) collective-permute-start(bf16[352,128]{1,0:T(8,128)(2,1)S(1)} %get-tuple-element.25), channel_id=1, source_target_pairs={{0,384},{64,448},{128,256},{192,320},{256,128},{320,192},{384,0},{... | collective-permute-start | bytes 270344 | tf_op jit(solution)/shard_map/ppermute | solution.py:199
  46.2 12.0 %all-to-all-start.1 = ((bf16[4,16,4,896]{3,2,1,0:T(4,128)(2,1)}), bf16[4,16,4,896]{3,2,1,0:T(4,128)(2,1)S(1)}, u32[]{:S(2)}, u32[]{:S(2)}) async-start(bf16[4,16,4,896]{3,2,1,0:T(4,128)(2,1)} %broadcast_in_dim.8), calls=%async_computation.1 | async-start | bytes 917504 | tf_op jit(solution)/shard_map/all_to_all | solution.py:215
  55.3 0.8 copy-start
  58.2 25.4 %all-to-all-start.2 = ((bf16[32,2,4,896]{3,2,1,0:T(4,128)(2,1)}), bf16[32,2,4,896]{3,2,1,0:T(4,128)(2,1)S(1)}, u32[]{:S(2)}, u32[]{:S(2)}) async-start(bf16[32,2,4,896]{3,2,1,0:T(4,128)(2,1)} %bitcast.12), calls=%async_computation.2 | async-start | bytes 917504 | tf_op jit(solution)/shard_map/all_to_all | solution.py:215
  67.4 22.7 %copy-start.1 = (bf16[2,4,16,256]{3,2,1,0:T(8,128)(2,1)S(1)}, bf16[2,4,16,256]{3,2,1,0:T(8,128)(2,1)}, u32[]{:S(2)}) copy-start(bf16[2,4,16,256]{3,2,1,0:T(8,128)(2,1)} %inputs_ref.3) | copy-start | bytes 196612
  67.4 22.7 %copy-start.2 = (bf16[2,4,16,256]{3,2,1,0:T(8,128)(2,1)S(1)}, bf16[2,4,16,256]{3,2,1,0:T(8,128)(2,1)}, u32[]{:S(2)}) copy-start(bf16[2,4,16,256]{3,2,1,0:T(8,128)(2,1)} %cot_ref.3) | copy-start | bytes 196612
  70.7 19.3 %collective-permute-start.5 = (bf16[128,256]{1,0:T(8,128)(2,1)S(1)}, bf16[128,256]{1,0:T(8,128)(2,1)S(1)}, u32[]{:S(2)}, u32[]{:S(2)}) collective-permute-start(bf16[128,256]{1,0:T(8,128)(2,1)S(1)} %get-tuple-element.30), channel_id=1, source_target_pairs={{0,128},{64,192},{128,0},{192,64},{256,384},{320,448},{384,256},{4... | collective-permute-start | bytes 196616 | tf_op jit(solution)/shard_map/ppermute | solution.py:199
  73.4 16.7 %collective-permute-start.6 = (bf16[128,256]{1,0:T(8,128)(2,1)S(1)}, bf16[128,256]{1,0:T(8,128)(2,1)S(1)}, u32[]{:S(2)}, u32[]{:S(2)}) collective-permute-start(bf16[128,256]{1,0:T(8,128)(2,1)S(1)} %get-tuple-element.31), channel_id=1, source_target_pairs={{0,256},{64,320},{128,384},{192,448},{256,0},{320,64},{384,128},{4... | collective-permute-start | bytes 196616 | tf_op jit(solution)/shard_map/ppermute | solution.py:199
  78.7 11.4 %collective-permute-start.7 = (bf16[128,256]{1,0:T(8,128)(2,1)S(1)}, bf16[128,256]{1,0:T(8,128)(2,1)S(1)}, u32[]{:S(2)}, u32[]{:S(2)}) collective-permute-start(bf16[128,256]{1,0:T(8,128)(2,1)S(1)} %get-tuple-element.32), channel_id=1, source_target_pairs={{0,384},{64,448},{128,256},{192,320},{256,128},{320,192},{384,0},{... | collective-permute-start | bytes 196616 | tf_op jit(solution)/shard_map/ppermute | solution.py:199
  83.8 9.5 %collective-permute-start.8 = (f32[4,896]{1,0:T(4,128)S(1)}, f32[4,896]{1,0:T(4,128)S(1)}, u32[]{:S(2)}, u32[]{:S(2)}) collective-permute-start(f32[4,896]{1,0:T(4,128)S(1)} %get-tuple-element.35), channel_id=1, source_target_pairs={{0,1},{1,0},{2,3},{3,2},{4,5},{5,4},{6,7},{7,6},{8,9},{9,8},{10,11... | collective-permute-start | bytes 43016 | tf_op jit(solution)/shard_map/ppermute | solution.py:281
